TPU v7x, 128 devices: a whole 4x4x4 slice. The times are simulated.
128 devices in a mesh: req: 8 (over z, core), exp: 16 (over y, x).
Axes of the slice: x: 4, y: 4, z: 4, core: 2. Of those that a mesh axis runs over, the one named last changes fastest.
Arguments:
- hidden_in: bfloat16 [16, 16, 64, 2048], P('exp', 'req'), may hold values from -6 to 6
- router_choice: int32 [16, 16, 64, 2], P('exp', 'req'), may hold values from 0 to 7, all different within a row; in each aligned block of 128 rows (0 to 127, 128 to 255, ..., all dimensions but the last counted through in order) at most 48 rows name the same one
- w_router: bfloat16 [2048, 8], replicated, may hold values from -0.125 to 0.125
- w_kv: bfloat16 [2048, 2048], replicated, may hold values from -0.125 to 0.125
- w_query: bfloat16 [16, 2048, 512], P('exp'), may hold values from -0.125 to 0.125
- w_out: bfloat16 [16, 512, 2048], P('exp'), may hold values from -0.75 to 0.75
- kv_cache: bfloat16 [16, 128, 128, 2048], P('exp', 'req'), may hold values from -68 to 68
- page_count: int32 [16, 16], P('exp'), may hold values from 1 to 32, 128 in all within a row
- tail_len: int32 [16, 16], P('exp'), may hold values from 1 to 128
- page_perm: int32 [16, 128], P('exp'), may hold values from 0 to 127, each once within a row
- parents: int32 [16, 16, 64], P('exp', 'req'), may hold values from 0 to 62, as said below
- accepted_leaf: int32 [16, 16], P('exp', 'req'), may hold values from 0 to 63
Outputs:
- attn_out: bfloat16 [16, 16, 64, 2048], P('exp', 'req')
- cache_rows: bfloat16 [16, 16, 64, 2048], P('exp', 'req')
Inputs may be any that keep to these rules, and one draw needn't show every extreme that they name: `router_choice`: in the rows of one device (aligned blocks of 128 rows), no expert is named by more than 48 rows, and 48 is reached. `page_count`: each row sums to 128; its largest entry is 32. `page_perm`: each row holds each number once. parents of token 0 is 0; for j >= 1 parents of token j is below j; the last token's parent is token 62.
All inputs are finite; a program needn't handle non-finite values.
Results may differ from a plain program's by a relative error of at most 0.014.
The roundings to bfloat16 on the way count: a program that leaves them out, or rounds other values in their place, can miss the bound.
Values may be sent and summed in bfloat16 or wider, within the bound.
A program may use at most 128 MiB of HBM per device.

v0:
```python
import jax
import jax.numpy as jnp
from jax import lax
from jax.sharding import PartitionSpec as P

D = 2048
HD = 128
EXPERTS = 8
KVH = 8
TOPK = 2
PAGE = 128
DRAFT = 64
REQ_X = 2
SLOTS = 16
CAP = 48


NEGATIVE_FILL = -1e30
NORM_EPSILON = 1e-06


def rotate(values_in, positions):
    half_width = values_in.shape[-1] // 2
    inverse_freq = 10000.0 ** (-jnp.arange(half_width, dtype=jnp.float32) / half_width)
    angles = positions.astype(jnp.float32)[..., None, None] * inverse_freq
    cosine_part = jnp.cos(angles)
    sine_part = jnp.sin(angles)
    leading = values_in[..., :half_width]
    trailing = values_in[..., half_width:]
    return jnp.concatenate(
        [
            leading * cosine_part - trailing * sine_part,
            trailing * cosine_part + leading * sine_part,
        ],
        axis=-1,
    )


def ancestry(parent_ids):
    count_tokens = parent_ids.shape[-1]
    index_row = jnp.arange(count_tokens, dtype=jnp.int32)
    linked = (parent_ids[..., :, None] == index_row) & (index_row[:, None] > 0)
    reachable = linked.astype(jnp.float32) + jnp.eye(count_tokens, dtype=jnp.float32)
    for doubling in range(count_tokens.bit_length()):
        reachable = jnp.minimum(
            jnp.matmul(reachable, reachable, precision=lax.Precision.HIGHEST), 1.0
        )
    return reachable


def block_partial(scores, valid, values):
    masked = jnp.where(valid, scores, NEGATIVE_FILL)
    block_max = jnp.max(masked, axis=-1)
    weights = jnp.where(valid, jnp.exp(masked - block_max[..., None]), 0.0)
    block_sum = jnp.sum(weights, axis=-1)
    block_acc = jnp.einsum(
        "bhqk,bkhd->bqhd", weights.astype(jnp.bfloat16), values, preferred_element_type=jnp.float32
    )
    return (block_max, block_sum, block_acc)


def merge_blocks(member, block_max, block_sum, block_acc):
    chosen = member[:, :, None, None]
    group_max = jnp.max(jnp.where(chosen, block_max[None], NEGATIVE_FILL), axis=1)
    scale_all = jnp.where(chosen, jnp.exp(block_max[None] - group_max[:, None]), 0.0)
    group_sum = jnp.sum(scale_all * block_sum[None], axis=1)
    group_acc = jnp.einsum("gshq,sqhd->gqhd", scale_all, block_acc, precision=lax.Precision.HIGHEST)
    present = group_sum > 0.0
    safe_sum = jnp.where(present, group_sum, 1.0)
    present_t = jnp.swapaxes(present, 1, 2)[..., None]
    out_values = jnp.where(
        present_t, group_acc / jnp.swapaxes(safe_sum, 1, 2)[..., None], 0.0
    ).astype(jnp.bfloat16)
    group_lse = jnp.where(present, group_max + jnp.log(safe_sum), NEGATIVE_FILL)
    return (out_values, jnp.swapaxes(group_lse, 1, 2))


def body(
    hidden_in,
    router_choice,
    w_router,
    w_kv,
    w_query,
    w_out,
    kv_cache,
    page_count,
    tail_len,
    page_perm,
    parents,
    accepted_leaf,
):
    split_count = lax.axis_size("exp") // EXPERTS
    holder_count = lax.axis_size("req")
    head_width = KVH * HD
    part_width = w_query.shape[2]
    group_requests = page_count.shape[1]
    pool_size = page_perm.shape[1]
    rows_dev = REQ_X * DRAFT
    pairs_dev = rows_dev * TOPK
    query_rows = DRAFT * TOPK
    scale_factor = HD ** (-0.5)
    tokens = hidden_in.reshape(rows_dev, D).astype(jnp.float32)
    normed = (
        tokens * lax.rsqrt(jnp.mean(tokens * tokens, axis=-1, keepdims=True) + NORM_EPSILON)
    ).astype(jnp.bfloat16)
    logits = jnp.dot(normed, w_router, preferred_element_type=jnp.float32)
    picked = router_choice.reshape(rows_dev, TOPK)
    gate_values = jax.nn.softmax(jnp.take_along_axis(logits, picked, axis=1), axis=-1)
    reachable = ancestry(parents[0])
    depth_of = (jnp.sum(reachable, axis=-1) - 1.0).astype(jnp.int32)
    owner_index = lax.axis_index("req")
    counts_all = page_count[0]
    lengths_all = (counts_all - 1) * PAGE + tail_len[0]
    own_lengths = lax.dynamic_slice_in_dim(lengths_all, owner_index * REQ_X, REQ_X)
    positions = own_lengths[:, None] + depth_of
    projected = jnp.dot(normed, w_kv, preferred_element_type=jnp.float32).reshape(
        REQ_X, DRAFT, 2, KVH, HD
    )
    new_keys = rotate(projected[:, :, 0], positions).astype(jnp.bfloat16)
    new_values = projected[:, :, 1].astype(jnp.bfloat16)
    new_kv = jnp.concatenate(
        [new_keys.reshape(REQ_X, DRAFT, head_width), new_values.reshape(REQ_X, DRAFT, head_width)],
        axis=-1,
    )
    pair_experts = picked.reshape(pairs_dev)
    onehot = (pair_experts[:, None] == jnp.arange(EXPERTS, dtype=jnp.int32)).astype(jnp.int32)
    slot_rank = jnp.sum((jnp.cumsum(onehot, axis=0) - onehot) * onehot, axis=1)
    target = pair_experts * CAP + slot_rank
    dispatch = (target[:, None] == jnp.arange(EXPERTS * CAP, dtype=jnp.int32)).astype(jnp.bfloat16)
    dispatch_three = dispatch.reshape(pairs_dev, EXPERTS, CAP)
    row_dispatch = jnp.sum(dispatch.reshape(rows_dev, TOPK, EXPERTS * CAP), axis=1)
    routed_rows = (
        jnp.einsum("re,rd->ed", row_dispatch, normed, preferred_element_type=jnp.float32)
        .astype(jnp.bfloat16)
        .reshape(EXPERTS, CAP, D)
    )
    copies = jnp.broadcast_to(routed_rows[:, None], (EXPERTS, split_count, CAP, D)).reshape(
        EXPERTS * split_count, CAP, D
    )
    raw_part = jnp.einsum(
        "scd,df->scf",
        lax.all_to_all(copies, "exp", split_axis=0, concat_axis=0, tiled=True),
        w_query[0],
        preferred_element_type=jnp.float32,
    ).astype(jnp.bfloat16)
    query_back = lax.all_to_all(raw_part, "exp", split_axis=0, concat_axis=0, tiled=True)
    query_parts = query_back.reshape(EXPERTS, split_count, CAP, part_width)
    raw_queries = jnp.einsum(
        "pec,ejch->pjh", dispatch_three, query_parts, preferred_element_type=jnp.float32
    )
    raw_queries = raw_queries.reshape(REQ_X, DRAFT, TOPK, KVH, HD)
    queries = rotate(raw_queries, positions[:, :, None]).astype(jnp.bfloat16)
    shared = lax.all_gather(
        queries.reshape(REQ_X, query_rows, head_width), "req", axis=0, tiled=True
    )
    ends = jnp.cumsum(counts_all)
    starts = ends - counts_all
    mine = owner_index * SLOTS + jnp.arange(SLOTS, dtype=jnp.int32)
    found = page_perm[0][None, :] == mine[:, None]
    page_pos = jnp.sum(jnp.where(found, jnp.arange(pool_size, dtype=jnp.int32)[None, :], 0), axis=1)
    slot_request = jnp.sum((ends[None, :] <= page_pos[:, None]).astype(jnp.int32), axis=1)
    member = slot_request[None, :] == jnp.arange(group_requests, dtype=jnp.int32)[:, None]
    page_start = jnp.sum(jnp.where(member, starts[:, None], 0), axis=0)
    page_length = jnp.sum(jnp.where(member, lengths_all[:, None], 0), axis=0)
    page_number = page_pos - page_start
    slot_queries = jnp.take(shared, slot_request, axis=0).reshape(SLOTS, query_rows, KVH, HD)
    cache_local = kv_cache[0]
    page_keys = cache_local[..., :head_width].reshape(SLOTS, PAGE, KVH, HD)
    page_values = cache_local[..., head_width:].reshape(SLOTS, PAGE, KVH, HD)
    scores = (
        jnp.einsum("sqhd,skhd->shqk", slot_queries, page_keys, preferred_element_type=jnp.float32)
        * scale_factor
    )
    key_pos = page_number[:, None] * PAGE + jnp.arange(PAGE, dtype=jnp.int32)
    key_valid = key_pos < page_length[:, None]
    slot_max, slot_sum, slot_acc = block_partial(scores, key_valid[:, None, None, :], page_values)
    held_out, held_lse = merge_blocks(member, slot_max, slot_sum, slot_acc)
    send_out = held_out.reshape(holder_count, REQ_X, query_rows, head_width)
    send_lse = held_lse.reshape(holder_count, REQ_X, query_rows, KVH)
    home_out = lax.all_to_all(send_out, "req", split_axis=0, concat_axis=0, tiled=True)
    home_lse = lax.all_to_all(send_lse, "req", split_axis=0, concat_axis=0, tiled=True)
    query_flat = queries.reshape(REQ_X, query_rows, KVH, HD)
    tree_scores = (
        jnp.einsum("rqhd,rkhd->rhqk", query_flat, new_keys, preferred_element_type=jnp.float32)
        * scale_factor
    )
    tree_valid = jnp.repeat(reachable, TOPK, axis=1)[:, None] > 0.5
    tree_max, tree_sum, tree_acc = block_partial(tree_scores, tree_valid, new_values)
    tree_out, tree_lse = merge_blocks(jnp.eye(REQ_X, dtype=bool), tree_max, tree_sum, tree_acc)
    all_lse = jnp.concatenate([home_lse, tree_lse[None]], axis=0)
    all_out = jnp.concatenate(
        [
            home_out.astype(jnp.float32).reshape(holder_count, REQ_X, query_rows, KVH, HD),
            tree_out.astype(jnp.float32)[None],
        ],
        axis=0,
    )
    top_lse = jnp.max(all_lse, axis=0)
    part_weight = jnp.exp(all_lse - top_lse)
    mixed_out = (
        jnp.sum(part_weight[..., None] * all_out, axis=0) / jnp.sum(part_weight, axis=0)[..., None]
    )
    attended = mixed_out.astype(jnp.bfloat16).reshape(pairs_dev, split_count, part_width)
    routed_out = jnp.einsum(
        "pec,pjh->ejch", dispatch_three, attended, preferred_element_type=jnp.float32
    )
    routed_out = routed_out.astype(jnp.bfloat16).reshape(EXPERTS * split_count, CAP, part_width)
    expert_part = jnp.einsum(
        "sch,hd->scd",
        lax.all_to_all(routed_out, "exp", split_axis=0, concat_axis=0, tiled=True),
        w_out[0],
        preferred_element_type=jnp.float32,
    ).astype(jnp.bfloat16)
    out_returned = lax.all_to_all(expert_part, "exp", split_axis=0, concat_axis=0, tiled=True)
    pair_out = jnp.einsum(
        "pec,ejcd->pjd",
        dispatch_three,
        out_returned.reshape(EXPERTS, split_count, CAP, D),
        preferred_element_type=jnp.float32,
    )
    pair_out = jnp.sum(pair_out, axis=1)
    combined = jnp.sum(pair_out.reshape(rows_dev, TOPK, D) * gate_values[..., None], axis=1)
    attn_out = combined.astype(jnp.bfloat16).reshape(1, REQ_X, DRAFT, D)
    leaf_row = jnp.take_along_axis(reachable, accepted_leaf[0][:, None, None], axis=1)[:, 0, :]
    selector = (
        leaf_row[:, None, :]
        * (depth_of[:, None, :] == jnp.arange(DRAFT, dtype=jnp.int32)[:, None]).astype(jnp.float32)
    ).astype(jnp.bfloat16)
    cache_rows = jnp.einsum(
        "rdj,rjc->rdc", selector, new_kv, preferred_element_type=jnp.float32
    ).astype(jnp.bfloat16)[None]
    return (attn_out, cache_rows)


def solution(mesh):
    placed = (
        P("exp", "req", None, None),
        P("exp", "req", None, None),
        P(),
        P(),
        P("exp", None, None),
        P("exp", None, None),
        P("exp", "req", None, None),
        P("exp", None),
        P("exp", None),
        P("exp", None),
        P("exp", "req", None),
        P("exp", "req"),
    )
    return jax.shard_map(
        body,
        mesh=mesh,
        in_specs=placed,
        out_specs=(P("exp", "req", None, None), P("exp", "req", None, None)),
        check_vma=False,
    )
```

profile of v0, /device:TPU:0, one launch (start us, length us, event | category | flops | bytes accessed | tf_op | source)
XLA Modules:
  0.0 402.5 jit_solution(4155768725178093252)
XLA Ops:
  16.6 7.2 %all-to-all-start = ((bf16[16,48,2048]{2,1,0:T(8,128)(2,1)}), bf16[16,48,2048]{2,1,0:T(8,128)(2,1)}, u32[]{:S(2)}, u32[]{:S(2)}) async-start(bf16[16,48,2048]{2,1,0:T(8,128)(2,1)} %bitcast.205), calls=%async_computation | async-start | bytes 6291456 | tf_op jit(solution)/shard_map/all_to_all | solution.py:142
  25.6 45.6 %all-to-all-done = bf16[16,48,2048]{2,1,0:T(8,128)(2,1)} async-done(((bf16[16,48,2048]{2,1,0:T(8,128)(2,1)}), bf16[16,48,2048]{2,1,0:T(8,128)(2,1)}, u32[]{:S(2)}, u32[]{:S(2)}) %all-to-all-start) | async-done | bytes 3145760 | tf_op jit(solution)/shard_map/all_to_all | solution.py:142
  71.3 5.2 %fusion.31 = bf16[16,48,512]{2,1,0:T(8,128)(2,1)} fusion(bf16[16,48,2048]{2,1,0:T(8,128)(2,1)} %all-to-all-done, bf16[1,2048,512]{2,1,0:T(8,128)(2,1)} %param.16), kind=kOutput, calls=%fused_computation.41 | convolution fusion | flops 1611005952 | bytes 6029312 | tf_op jit(solution)/shard_map/scd,df->scf/dot_general | solution.py:140
  81.6 12.5 %all-to-all-done.1 = bf16[16,48,512]{2,1,0:T(8,128)(2,1)S(1)} async-done(((bf16[16,48,512]{2,1,0:T(8,128)(2,1)}), bf16[16,48,512]{2,1,0:T(8,128)(2,1)S(1)}, u32[]{:S(2)}, u32[]{:S(2)}) %all-to-all-start.1) | async-done | bytes 786464 | tf_op jit(solution)/shard_map/all_to_all | solution.py:146
  103.1 12.4 %copy.397 = bf16[2048,2048]{1,0:T(8,128)(2,1)} copy(bf16[2048,2048]{0,1:T(8,128)(2,1)} %bitcast.206) | data formatting | bytes 16777216 | tf_op jit(solution)/shard_map/dot_general | solution.py:116
  115.5 12.3 %copy.346 = bf16[1,16,128,2048]{2,3,1,0:T(8,128)(2,1)} copy(bf16[1,16,128,2048]{3,2,1,0:T(8,128)(2,1)} %param.18) | data formatting | bytes 16777216 | tf_op args[6]
  128.4 7.0 %fusion.110 = (bf16[16,128,1024]{1,2,0:T(8,128)(2,1)}, bf16[16,128,1024]{1,2,0:T(8,128)(2,1)}) fusion(bf16[16,128,2048]{1,2,0:T(8,128)(2,1)} %bitcast.202), kind=kLoop, calls=%fused_computation.205 | loop fusion | bytes 16777216 | tf_op jit(solution)/shard_map/slice | solution.py:169
  140.3 4.9 %gather_fusion = bf16[16,128,1024]{2,1,0:T(8,128)(2,1)} fusion(bf16[16,128,1024]{2,1,0:T(8,128)(2,1)} %all-gather.2.cloned.1.call-done, s32[1024]{0:T(1024)S(1)} %pad_clamp_fusion), kind=kCustom, calls=%fused_computation | custom fusion | bytes 8388672 | tf_op jit(solution)/shard_map/jit(_take)/gather | solution.py:166
  145.2 6.4 %copy.345 = bf16[16,128,1024]{1,2,0:T(8,128)(2,1)} copy(bf16[16,128,1024]{2,1,0:T(8,128)(2,1)} %gather_fusion) | data formatting | bytes 8388608 | tf_op jit(solution)/shard_map/jit(_take)/gather | solution.py:166
  151.6 8.8 %fusion.4 = (f32[16,8,128]{2,1,0:T(8,128)S(1)}, f32[16,8,128,128]{2,3,1,0:T(8,128)}) fusion(pred[16,128]{1,0:T(8,128)(4,1)S(1)} %add_compare_fusion, bf16[16,128,8,128]{1,3,2,0:T(8,128)(2,1)} %bitcast.209, bf16[16,128,8,128]{1,3,2,0:T(8,128)(2,1)} %bitcast.208, pred[16]{0:T(512)(128)(4,1)S(1)} %compare_and_fusion.1), kind=kOutput, calls=%fused_computation.14 | convolution fusion | flops 545243136 | bytes 16844816 | tf_op jit(solution)/shard_map/sqhd,skhd->shqk/dot_general | solution.py:171
  161.4 5.3 %fusion.6 = f32[16,8,128]{2,1,0:T(8,128)S(1)} fusion(f32[16,8,128,128]{2,3,1,0:T(8,128)} %get-tuple-element.29, f32[16,8,128]{2,1,0:T(8,128)S(1)} %get-tuple-element.28, pred[16,128]{1,0:T(8,128)(4,1)S(1)} %add_compare_fusion), kind=kLoop, calls=%fused_computation.16 | loop fusion | flops 10469376 | bytes 8521728 | tf_op jit(solution)/shard_map/reduce_sum | solution.py:55
  166.8 10.5 %fusion.21 = f32[16,128,8,128]{3,1,2,0:T(8,128)} fusion(bf16[16,128,8,128]{1,3,2,0:T(8,128)(2,1)S(1)} %bitcast.204, f32[16,8,128,128]{2,3,1,0:T(8,128)} %get-tuple-element.29, f32[16,8,128]{2,1,0:T(8,128)S(1)} %get-tuple-element.28, pred[16,128]{1,0:T(8,128)(4,1)S(1)} %add_compare_fusion), kind=kOutput, calls=%fused_computation.32 | convolution fusion | flops 547356672 | bytes 21039104 | tf_op jit(solution)/shard_map/bhqk,bkhd->bqhd/dot_general | solution.py:56
  181.6 29.5 %multiply_reduce_fusion.1 = f32[16,8,128]{0,1,2:T(8,128)S(1)} fusion(f32[16,8,128]{0,1,2:T(8,128)} %copy.350, f32[16,8,128]{0,1,2:T(8,128)S(1)} %select_reduce_fusion, f32[16,8,128]{0,1,2:T(8,128)} %copy.349, pred[16,16]{1,0:T(8,128)(4,1)S(1)} %iota_compare_fusion.4), kind=kLoop, calls=%fused_computation.9 | loop fusion | flops 1032192 | bytes 262400 | tf_op jit(solution)/shard_map/reduce_sum | solution.py:66
  215.8 5.2 %all-to-all-start.2 = ((f32[8,2,128,8]{2,3,1,0:T(8,128)}), f32[8,2,128,8]{2,3,1,0:T(8,128)S(1)}, u32[]{:S(2)}, u32[]{:S(2)}) async-start(f32[8,2,128,8]{2,3,1,0:T(8,128)} %bitcast.28), calls=%async_computation.2 | async-start | bytes 131072 | tf_op jit(solution)/shard_map/all_to_all | solution.py:181
  221.1 18.7 %fusion.1 = bf16[16,128,8,128]{3,0,2,1:T(8,128)(2,1)} fusion(f32[16,128,8]{0,2,1:T(8,128)} %bitcast_select_fusion, pred[16,128,8]{0,2,1:T(8,128)(4,1)S(1)} %get-tuple-element.11, f32[16,8,128]{0,1,2:T(8,128)} %copy-done.5, f32[16,8,128]{0,1,2:T(8,128)} %copy.349, pred[16,16]{1,0:T(8,128)(4,1)S(1)} %iota_compare_fusion.4, f32[16,128,8,128]{3,1,2,0:T(8,128)} %fusion.21), kind=kOutput, calls=%fused_computation.6 | convolution fusion | flops 409468928 | bytes 12796160 | tf_op jit(solution)/shard_map/gshq,sqhd->gqhd/dot_general | solution.py:67
  239.8 6.6 %copy.365 = bf16[16,128,8,128]{1,3,2,0:T(8,128)(2,1)} copy(bf16[16,128,8,128]{3,0,2,1:T(8,128)(2,1)} %fusion.1) | data formatting | bytes 8388608 | tf_op jit(solution)/shard_map/convert_element_type | solution.py:73
  246.4 5.3 %all-to-all-start.3 = ((bf16[8,2,128,1024]{2,3,1,0:T(8,128)(2,1)}), bf16[8,2,128,1024]{2,3,1,0:T(8,128)(2,1)}, u32[]{:S(2)}, u32[]{:S(2)}) async-start(bf16[8,2,128,1024]{2,3,1,0:T(8,128)(2,1)} %bitcast.203), calls=%async_computation.3 | async-start | bytes 8388608 | tf_op jit(solution)/shard_map/all_to_all | solution.py:180
  270.7 4.9 %multiply_reduce_fusion.3 = f32[2,8,128]{0,1,2:T(8,128)} fusion(pred[2,2]{1,0:T(4,128)(4,1)S(1)} %iota_compare_fusion.7, f32[2,8,128]{0,1,2:T(8,128)} %copy.359, f32[2,8,128]{0,1,2:T(8,128)} %select_reduce_fusion.1, f32[2,8,128]{0,1,2:T(8,128)} %copy.358), kind=kLoop, calls=%fused_computation.61 | loop fusion | flops 14336 | bytes 32772 | tf_op jit(solution)/shard_map/reduce_sum | solution.py:66
  278.8 10.4 %fusion.38 = bf16[1,2,128,8,128]{4,1,3,2,0:T(2,128)(2,1)} fusion(f32[2,128,8,128]{3,0,2,1:T(2,128)} %copy.367, pred[2,128,8]{0,2,1:T(8,128)(4,1)} %copy.366, pred[2,2]{1,0:T(4,128)(4,1)} %copy-done.20, f32[2,128,8]{0,2,1:T(8,128)} %copy.368, f32[2,8,128]{0,1,2:T(8,128)} %select_reduce_fusion.1, f32[2,8,128]{0,1,2:T(8,128)} %copy.358), kind=kOutput, calls=%fused_computation.68 | convolution fusion | flops 7086080 | bytes 1599492 | tf_op jit(solution)/shard_map/gshq,sqhd->gqhd/dot_general | solution.py:67
  291.9 9.5 %all-to-all-done.3 = bf16[8,2,128,1024]{2,3,1,0:T(8,128)(2,1)} async-done(((bf16[8,2,128,1024]{2,3,1,0:T(8,128)(2,1)}), bf16[8,2,128,1024]{2,3,1,0:T(8,128)(2,1)}, u32[]{:S(2)}, u32[]{:S(2)}) %all-to-all-start.3) | async-done | bytes 4194336 | tf_op jit(solution)/shard_map/all_to_all | solution.py:180
  311.7 17.4 %all_to_all.30 = bf16[16,48,512]{2,1,0:T(8,128)(2,1)S(1)} all-to-all(bf16[16,48,512]{2,1,0:T(8,128)(2,1)S(1)} %bitcast.213), channel_id=1, replica_groups=mesh['req'=8,'exp'=16] {'exp'}, dimensions={0} | all-to-all | bytes 1572864 | tf_op jit(solution)/shard_map/all_to_all | solution.py:210
  332.6 4.8 %all-to-all-start.5 = ((bf16[16,48,2048]{2,1,0:T(8,128)(2,1)}), bf16[16,48,2048]{2,1,0:T(8,128)(2,1)}, u32[]{:S(2)}, u32[]{:S(2)}) async-start(bf16[16,48,2048]{2,1,0:T(8,128)(2,1)} %convolution_convert_fusion), calls=%async_computation.5 | async-start | bytes 6291456 | tf_op jit(solution)/shard_map/all_to_all | solution.py:214
  349.8 31.8 %all-to-all-done.5 = bf16[16,48,2048]{2,1,0:T(8,128)(2,1)} async-done(((bf16[16,48,2048]{2,1,0:T(8,128)(2,1)}), bf16[16,48,2048]{2,1,0:T(8,128)(2,1)}, u32[]{:S(2)}, u32[]{:S(2)}) %all-to-all-start.5) | async-done | bytes 3145760 | tf_op jit(solution)/shard_map/all_to_all | solution.py:214
  389.9 5.6 %multiply_reduce_fusion.2 = bf16[128,2048]{1,0:T(8,128)(2,1)} fusion(f32[128,2,2048]{2,1,0:T(2,128)} %reshape.619, f32[128,2]{1,0:T(8,128)S(1)} %copy.378), kind=kLoop, calls=%fused_computation.39 | loop fusion | flops 786432 | bytes 2622464 | tf_op jit(solution)/shard_map/reduce_sum | solution.py:222
  (189 shorter events, 99.8 us)
Async XLA Ops:
  7.2 321.9 %copy-start = (bf16[1,512,2048]{2,1,0:T(8,128)(2,1)S(1)}, bf16[1,512,2048]{2,1,0:T(8,128)(2,1)}, u32[]{:S(2)}) copy-start(bf16[1,512,2048]{2,1,0:T(8,128)(2,1)} %param.17) | copy-start | bytes 6291460
  10.5 6.1 %copy-start.18 = (s32[128,2]{0,1:T(2,128)}, s32[128,2]{0,1:T(2,128)S(1)}, u32[]{:S(2)}) copy-start(s32[128,2]{0,1:T(2,128)S(1)} %reshape_reshape.6) | copy-start | bytes 3076
  14.4 9.5 %copy-start.21 = (s32[1,16]{1,0:T(1,128)S(1)}, s32[1,16]{1,0:T(1,128)}, u32[]{:S(2)}) copy-start(s32[1,16]{1,0:T(1,128)} %param.19) | copy-start | bytes 196
  14.4 9.8 %copy-start.22 = (s32[1,16]{1,0:T(1,128)S(1)}, s32[1,16]{1,0:T(1,128)}, u32[]{:S(2)}) copy-start(s32[1,16]{1,0:T(1,128)} %param.20) | copy-start | bytes 196
  14.4 9.9 %copy-start.23 = (s32[1,2,64]{2,1,0:T(2,128)S(1)}, s32[1,2,64]{2,1,0:T(2,128)}, u32[]{:S(2)}) copy-start(s32[1,2,64]{2,1,0:T(2,128)} %param.22) | copy-start | bytes 1540
  16.6 54.7 %all-to-all-start = ((bf16[16,48,2048]{2,1,0:T(8,128)(2,1)}), bf16[16,48,2048]{2,1,0:T(8,128)(2,1)}, u32[]{:S(2)}, u32[]{:S(2)}) async-start(bf16[16,48,2048]{2,1,0:T(8,128)(2,1)} %bitcast.205), calls=%async_computation | async-start | bytes 6291456 | tf_op jit(solution)/shard_map/all_to_all | solution.py:142
  76.5 17.6 %all-to-all-start.1 = ((bf16[16,48,512]{2,1,0:T(8,128)(2,1)}), bf16[16,48,512]{2,1,0:T(8,128)(2,1)S(1)}, u32[]{:S(2)}, u32[]{:S(2)}) async-start(bf16[16,48,512]{2,1,0:T(8,128)(2,1)} %fusion.31), calls=%async_computation.1 | async-start | bytes 1572864 | tf_op jit(solution)/shard_map/all_to_all | solution.py:146
  80.9 59.4 %all-gather.2.cloned.1.call-start = ((), (), s32[]{:S(2)}) async-start(), calls=%async_computation.6 | async-start | bytes 4718592 | tf_op jit(solution)/shard_map/all_gather | solution.py:153
  81.2 19.5 %copy-start.17 = (f32[2,64]{1,0:T(2,128)}, f32[2,64]{1,0:T(2,128)S(1)}, u32[]{:S(2)}) copy-start(f32[2,64]{1,0:T(2,128)S(1)} %get-tuple-element.24) | copy-start | bytes 1540
  81.2 21.0 %copy-start.11 = (f32[2,64,64]{2,1,0:T(8,128)}, f32[2,64,64]{2,1,0:T(8,128)S(1)}, u32[]{:S(2)}) copy-start(f32[2,64,64]{2,1,0:T(8,128)S(1)} %get-tuple-element.25) | copy-start | bytes 98308
  81.6 19.1 %copy-start.10 = (f32[2,64,64]{2,1,0:T(8,128)}, f32[2,64,64]{2,1,0:T(8,128)S(1)}, u32[]{:S(2)}) copy-start(f32[2,64,64]{2,1,0:T(8,128)S(1)} %get-tuple-element.21) | copy-start | bytes 98308
  115.5 12.3 %copy-start.24 = (s32[1,128]{1,0:T(1,128)S(1)}, s32[1,128]{1,0:T(1,128)}, u32[]{:S(2)}) copy-start(s32[1,128]{1,0:T(1,128)} %param.21) | copy-start | bytes 1540
  128.4 8.8 %copy-start.1 = (bf16[2048,2048]{1,0:T(8,128)(2,1)S(1)}, bf16[2048,2048]{1,0:T(8,128)(2,1)}, u32[]{:S(2)}) copy-start(bf16[2048,2048]{1,0:T(8,128)(2,1)} %copy.397) | copy-start | bytes 25165828
  128.4 8.9 %copy-start.8 = (bf16[1,2,64,2048]{3,2,1,0:T(8,128)(2,1)S(1)}, bf16[1,2,64,2048]{3,2,1,0:T(8,128)(2,1)}, u32[]{:S(2)}) copy-start(bf16[1,2,64,2048]{3,2,1,0:T(8,128)(2,1)} %param.12) | copy-start | bytes 1572868
  161.4 5.3 %copy-start.2 = (bf16[16,128,1024]{1,2,0:T(8,128)(2,1)S(1)}, bf16[16,128,1024]{1,2,0:T(8,128)(2,1)}, u32[]{:S(2)}) copy-start(bf16[16,128,1024]{1,2,0:T(8,128)(2,1)} %get-tuple-element.12) | copy-start | bytes 12582916
  181.6 29.5 %copy-start.5 = (f32[16,8,128]{0,1,2:T(8,128)}, f32[16,8,128]{0,1,2:T(8,128)S(1)}, u32[]{:S(2)}) copy-start(f32[16,8,128]{0,1,2:T(8,128)S(1)} %select_reduce_fusion) | copy-start | bytes 196612
  215.8 30.6 %all-to-all-start.2 = ((f32[8,2,128,8]{2,3,1,0:T(8,128)}), f32[8,2,128,8]{2,3,1,0:T(8,128)S(1)}, u32[]{:S(2)}, u32[]{:S(2)}) async-start(f32[8,2,128,8]{2,3,1,0:T(8,128)} %bitcast.28), calls=%async_computation.2 | async-start | bytes 131072 | tf_op jit(solution)/shard_map/all_to_all | solution.py:181
  246.4 55.0 %all-to-all-start.3 = ((bf16[8,2,128,1024]{2,3,1,0:T(8,128)(2,1)}), bf16[8,2,128,1024]{2,3,1,0:T(8,128)(2,1)}, u32[]{:S(2)}, u32[]{:S(2)}) async-start(bf16[8,2,128,1024]{2,3,1,0:T(8,128)(2,1)} %bitcast.203), calls=%async_computation.3 | async-start | bytes 8388608 | tf_op jit(solution)/shard_map/all_to_all | solution.py:180
  251.7 5.4 %copy-start.12 = (pred[2,128,64]{1,2,0:T(8,128)(4,1)S(1)}, pred[2,128,64]{1,2,0:T(8,128)(4,1)}, u32[]{:S(2)}) copy-start(pred[2,128,64]{1,2,0:T(8,128)(4,1)} %copy.352) | copy-start | bytes 49156
  251.7 19.0 %copy-start.20 = (pred[2,2]{1,0:T(4,128)(4,1)}, pred[2,2]{1,0:T(4,128)(4,1)S(1)}, u32[]{:S(2)}) copy-start(pred[2,2]{1,0:T(4,128)(4,1)S(1)} %iota_compare_fusion.7) | copy-start | bytes 16
  256.9 7.4 %copy-start.13 = (pred[2,128,64]{1,2,0:T(8,128)(4,1)S(1)}, pred[2,128,64]{1,2,0:T(8,128)(4,1)}, u32[]{:S(2)}) copy-start(pred[2,128,64]{1,2,0:T(8,128)(4,1)} %copy.352) | copy-start | bytes 49156
  301.4 8.7 %copy-start.16 = (s32[8,48]{1,0:T(8,128)S(1)}, s32[8,48]{1,0:T(8,128)}, u32[]{:S(2)}) copy-start(s32[8,48]{1,0:T(8,128)} %multiply_add_fusion.2) | copy-start | bytes 4612
  301.4 8.7 %copy-start.19 = (s32[256]{0:T(256)S(1)}, s32[256]{0:T(256)}, u32[]{:S(2)}) copy-start(s32[256]{0:T(256)} %multiply_add_fusion.4) | copy-start | bytes 3076
  332.6 49.0 %all-to-all-start.5 = ((bf16[16,48,2048]{2,1,0:T(8,128)(2,1)}), bf16[16,48,2048]{2,1,0:T(8,128)(2,1)}, u32[]{:S(2)}, u32[]{:S(2)}) async-start(bf16[16,48,2048]{2,1,0:T(8,128)(2,1)} %convolution_convert_fusion), calls=%async_computation.5 | async-start | bytes 6291456 | tf_op jit(solution)/shard_map/all_to_all | solution.py:214
  (7 other events, 16.9 us)
Sparse Core Ops, SparseCore 0:
  102.3 30.9 all-gather.1
where the time goes:
time: 410 us; the launch traced here: 402 us
  waiting for transfers between devices  99.4 us (24%)
  local copies, waits for them, and re-layouts  96.2 us (23%)
  matrix products  75.3 us (18%)
  other arithmetic  72.5 us (18%)
  starting transfers between devices  26.9 us (7%)
  blocking collectives  17.4 us (4%)
  between operations  14.9 us (4%)
    all_to_all x1, waiting for transfers between devices, body(): lax.all_to_all(copies, 'exp', split_axis=0, concat_axis=0, tiled=True)  45.6 us
    reduce_sum x2, other arithmetic, merge_blocks(): group_sum = jnp.sum(scale_all * block_sum[None], axis=1)  34.4 us
    all_to_all x1, waiting for transfers between devices, body(): lax.all_to_all(expert_part, 'exp', split_axis=0, concat_axis=0, tiled=True)  31.8 us
    dot_general x2, matrix products, merge_blocks(): jnp.einsum('gshq,sqhd->gqhd', scale_all, block_acc, precision=lax.Precisi...  29.1 us
    unnamed x54, local copies, waits for them, and re-layouts  17.6 us
    all_to_all x1, blocking collectives, body(): lax.all_to_all(routed_out, 'exp', split_axis=0, concat_axis=0, tiled=True)  17.4 us
    dot_general x2, matrix products, block_partial(): jnp.einsum('bhqk,bkhd->bqhd', weights.astype(jnp.bfloat16), values, prefe...  12.8 us
    all_to_all x1, waiting for transfers between devices, body(): lax.all_to_all(raw_part, 'exp', split_axis=0, concat_axis=0, tiled=True)  12.5 us
  transfers between devices with their start and end apart: 6, of which 4 were waited for; matrix products, arithmetic and copies ran while one was open for 29% of the time, Pallas kernels for 0%

commit v1 on v0

v1 whole, which is shorter than its diff:
```python
import jax
import jax.numpy as jnp
from jax import lax
from jax.experimental import pallas as pl
from jax.experimental.pallas import tpu as pltpu
from jax.sharding import PartitionSpec as P

D = 2048
HD = 128
EXPERTS = 8
KVH = 8
TOPK = 2
PAGE = 128
DRAFT = 64
REQ_X = 2
SLOTS = 16
CAP = 48
ROWS = REQ_X * DRAFT
QROWS = DRAFT * TOPK
HEADW = KVH * HD
BUF = EXPERTS * CAP

NEGATIVE_FILL = -1e30
NORM_EPSILON = 1e-06
SCALE = HD**-0.5
LOG2E = 1.4426950408889634
EXP_SCALE = SCALE * LOG2E
F32 = jnp.float32
BF16 = jnp.bfloat16
VMEM = pltpu.VMEM


def whole(shape):
    return pl.BlockSpec(shape, lambda *_: (0,) * len(shape))


def rotate_head(x, cos_full, sin_full):
    return x * cos_full + pltpu.roll(x, HD // 2, 1) * sin_full


def prologue_kernel(hidden_ref, choice_ref, choice_t_ref, router_ref, routed_ref, normed_ref, gates_ref, slots_ref):
    tokens = hidden_ref[...].astype(F32)
    mean_sq = jnp.mean(tokens * tokens, axis=-1, keepdims=True)
    normed = (tokens * lax.rsqrt(mean_sq + NORM_EPSILON)).astype(BF16)
    normed_ref[...] = normed
    logits = jnp.dot(normed, router_ref[...], preferred_element_type=F32)
    lane8 = lax.broadcasted_iota(jnp.int32, (ROWS, EXPERTS), 1)
    hot = [lane8 == choice_ref[:, t : t + 1] for t in range(TOPK)]
    picked = [jnp.sum(jnp.where(h, logits, 0.0), axis=1, keepdims=True) for h in hot]
    top = jnp.maximum(picked[0], picked[1])
    raised = [jnp.exp(p - top) for p in picked]
    total = raised[0] + raised[1]
    row_i = lax.broadcasted_iota(jnp.int32, (ROWS, ROWS), 0)
    col_i = lax.broadcasted_iota(jnp.int32, (ROWS, ROWS), 1)
    lower = (col_i < row_i).astype(F32).astype(BF16)
    both = (hot[0] | hot[1]).astype(F32).astype(BF16)
    before = jnp.dot(lower, both, preferred_element_type=F32)
    for t in range(TOPK):
        gates_ref[:, t : t + 1] = raised[t] / total
        rank = jnp.sum(jnp.where(hot[t], before, 0.0), axis=1, keepdims=True)
        slots_ref[:, t : t + 1] = choice_ref[:, t : t + 1] * CAP + rank.astype(jnp.int32)
    sub8 = lax.broadcasted_iota(jnp.int32, (EXPERTS, ROWS), 0)
    hot_t = [sub8 == choice_t_ref[t : t + 1, :] for t in range(TOPK)]
    upper = (row_i < col_i).astype(F32).astype(BF16)
    both_t = (hot_t[0] | hot_t[1]).astype(F32).astype(BF16)
    before_t = jnp.dot(both_t, upper, preferred_element_type=F32)
    slot_row = [
        choice_t_ref[t : t + 1, :] * CAP
        + jnp.sum(jnp.where(hot_t[t], before_t, 0.0), axis=0, keepdims=True).astype(jnp.int32)
        for t in range(TOPK)
    ]
    buf_i = lax.broadcasted_iota(jnp.int32, (BUF, ROWS), 0)
    spread = ((buf_i == slot_row[0]) | (buf_i == slot_row[1])).astype(F32).astype(BF16)
    for n in range(D // 512):
        cols = slice(n * 512, (n + 1) * 512)
        routed_ref[:, cols] = jnp.dot(spread, normed[:, cols], preferred_element_type=F32).astype(BF16)


def prologue(hidden, choice, w_router):
    return pl.pallas_call(
        prologue_kernel,
        out_shape=(
            jax.ShapeDtypeStruct((BUF, D), BF16),
            jax.ShapeDtypeStruct((ROWS, D), BF16),
            jax.ShapeDtypeStruct((ROWS, TOPK), F32),
            jax.ShapeDtypeStruct((ROWS, TOPK), jnp.int32),
        ),
        name="prologue",
    )(hidden, choice, choice.T, w_router)


def expert_query_kernel(parity_ref, rows_ref, own_ref, other_ref, out_ref):
    n = pl.program_id(0)

    @pl.when(n < 2)
    def _():
        out_ref[...] = jnp.dot(rows_ref[...], own_ref[...], preferred_element_type=F32).astype(BF16)

    @pl.when(n >= 2)
    def _():
        out_ref[...] = jnp.dot(rows_ref[...], other_ref[...], preferred_element_type=F32).astype(BF16)


def expert_query(parity, rows, w_own, w_other):
    width = w_own.shape[1] // 2
    return pl.pallas_call(
        expert_query_kernel,
        out_shape=jax.ShapeDtypeStruct((BUF, HEADW), BF16),
        grid_spec=pltpu.PrefetchScalarGridSpec(
            num_scalar_prefetch=1,
            grid=(4,),
            in_specs=[
                pl.BlockSpec((BUF, D), lambda n, par: (0, 0)),
                pl.BlockSpec((D, width), lambda n, par: (0, jnp.minimum(n, 1))),
                pl.BlockSpec((D, width), lambda n, par: (0, jnp.maximum(n - 2, 0))),
            ],
            out_specs=pl.BlockSpec(
                (BUF, width),
                lambda n, par: (0, jnp.where(n < 2, par[0] * 2 + n, (1 - par[0]) * 2 + n - 2)),
            ),
        ),
        name="expert_query",
    )(parity, rows, w_own, w_other)


def pick_rotate_kernel(slots_ref, cos_ref, sin_ref, back_ref, out_ref):
    buf_i = lax.broadcasted_iota(jnp.int32, (ROWS, BUF), 1)
    for t in range(TOPK):
        pick = (buf_i == slots_ref[:, t : t + 1]).astype(F32).astype(BF16)
        for h in range(KVH):
            cols = slice(h * HD, (h + 1) * HD)
            raw = jnp.dot(pick, back_ref[:, cols], preferred_element_type=F32)
            turned = rotate_head(raw, cos_ref[...], sin_ref[...]).astype(BF16)
            for r in range(REQ_X):
                out_ref[r, t * DRAFT : (t + 1) * DRAFT, cols] = turned[r * DRAFT : (r + 1) * DRAFT]


def pick_rotate(slots, cos_full, sin_full, back):
    return pl.pallas_call(
        pick_rotate_kernel,
        out_shape=jax.ShapeDtypeStruct((REQ_X, QROWS, HEADW), BF16),
        name="pick_rotate",
    )(slots, cos_full, sin_full, back)


def new_kv_kernel(normed_ref, weight_ref, cos_ref, sin_ref, out_ref):
    tile = jnp.dot(normed_ref[...], weight_ref[...], preferred_element_type=F32)
    n = pl.program_id(0)
    is_key = n < pl.num_programs(0) // 2

    @pl.when(is_key)
    def _():
        for h in range(tile.shape[1] // HD):
            cols = slice(h * HD, (h + 1) * HD)
            out_ref[:, cols] = rotate_head(tile[:, cols], cos_ref[...], sin_ref[...]).astype(BF16)

    @pl.when(jnp.logical_not(is_key))
    def _():
        out_ref[...] = tile.astype(BF16)


def project_kv(normed, w_kv, cos_full, sin_full):
    tile = 512
    return pl.pallas_call(
        new_kv_kernel,
        out_shape=jax.ShapeDtypeStruct((ROWS, 2 * HEADW), BF16),
        grid=(2 * HEADW // tile,),
        in_specs=[
            whole((ROWS, D)),
            pl.BlockSpec((D, tile), lambda n: (0, n)),
            whole((ROWS, HD)),
            whole((ROWS, HD)),
        ],
        out_specs=pl.BlockSpec((ROWS, tile), lambda n: (0, n)),
        cost_estimate=pl.CostEstimate(flops=2 * ROWS * D * D, bytes_accessed=2 * D * D, transcendentals=0),
        name="project_kv",
    )(normed, w_kv, cos_full, sin_full)


def columns_to_rows(columns):
    lane = lax.broadcasted_iota(jnp.int32, (QROWS, HD), 1)
    wide = jnp.zeros((QROWS, HD), F32)
    for h, column in enumerate(columns):
        wide = jnp.where(lane == h, column, wide)
    return wide.T[:KVH]


def page_kernel(order_ref, request_ref, valid_ref, query_ref, cache_ref, out_ref, lse_ref, max_ref, sum_ref, acc_ref):
    i = pl.program_id(0)
    last_i = pl.num_programs(0) - 1
    here = request_ref[i]
    starts = (i == 0) | (request_ref[jnp.maximum(i - 1, 0)] != here)
    finishes = (i == last_i) | (request_ref[jnp.minimum(i + 1, last_i)] != here)

    @pl.when(i == 0)
    def _():
        lse_ref[...] = jnp.full_like(lse_ref, NEGATIVE_FILL)

    @pl.when(starts)
    def _():
        max_ref[...] = jnp.full_like(max_ref, NEGATIVE_FILL)
        sum_ref[...] = jnp.zeros_like(sum_ref)
        acc_ref[...] = jnp.zeros_like(acc_ref)

    lane = lax.broadcasted_iota(jnp.int32, (QROWS, PAGE), 1)
    valid = lane < valid_ref[i]
    for h in range(KVH):
        cols = slice(h * HD, (h + 1) * HD)
        scores = lax.dot_general(
            query_ref[0, :, cols], cache_ref[0, :, cols], (((1,), (1,)), ((), ())), preferred_element_type=F32
        )
        scores = jnp.where(valid, scores, NEGATIVE_FILL)
        page_max = jnp.max(scores, axis=-1, keepdims=True)
        weights = jnp.exp2((scores - page_max) * EXP_SCALE)
        page_sum = jnp.sum(weights, axis=-1, keepdims=True)
        page_acc = jnp.dot(
            weights.astype(BF16), cache_ref[0, :, HEADW + h * HD : HEADW + (h + 1) * HD], preferred_element_type=F32
        )
        old_max = max_ref[h]
        new_max = jnp.maximum(old_max, page_max)
        old_scale = jnp.exp2((old_max - new_max) * EXP_SCALE)
        page_scale = jnp.exp2((page_max - new_max) * EXP_SCALE)
        max_ref[h] = new_max
        sum_ref[h] = sum_ref[h] * old_scale + page_sum * page_scale
        acc_ref[:, cols] = acc_ref[:, cols] * old_scale + page_acc * page_scale

    @pl.when(finishes)
    def _():
        columns = []
        for h in range(KVH):
            cols = slice(h * HD, (h + 1) * HD)
            total = sum_ref[h]
            out_ref[0, :, cols] = (acc_ref[:, cols] / total).astype(BF16)
            columns.append(max_ref[h] * SCALE + jnp.log(total))
        lse_ref[here] = columns_to_rows(columns)


def attend_pages(order, requests, valid, queries, cache):
    count = queries.shape[0]
    return pl.pallas_call(
        page_kernel,
        out_shape=(
            jax.ShapeDtypeStruct((count, QROWS, HEADW), BF16),
            jax.ShapeDtypeStruct((count, KVH, QROWS), F32),
        ),
        grid_spec=pltpu.PrefetchScalarGridSpec(
            num_scalar_prefetch=3,
            grid=(SLOTS,),
            in_specs=[
                pl.BlockSpec((1, QROWS, HEADW), lambda i, o, r, v: (r[i], 0, 0)),
                pl.BlockSpec((1, PAGE, 2 * HEADW), lambda i, o, r, v: (o[i], 0, 0)),
            ],
            out_specs=(
                pl.BlockSpec((1, QROWS, HEADW), lambda i, o, r, v: (r[i], 0, 0)),
                pl.BlockSpec((count, KVH, QROWS), lambda i, o, r, v: (0, 0, 0)),
            ),
            scratch_shapes=[VMEM((KVH, QROWS, 1), F32), VMEM((KVH, QROWS, 1), F32), VMEM((QROWS, HEADW), F32)],
        ),
        name="attend_pages",
    )(order, requests, valid, queries, cache)


def tree_kernel(query_ref, kv_ref, reach_ref, out_ref, lse_ref):
    for r in range(REQ_X):
        rows = slice(r * DRAFT, (r + 1) * DRAFT)
        reach = reach_ref[r]
        valid = jnp.concatenate([reach] * TOPK, axis=0) > 0.5
        columns = []
        for h in range(KVH):
            cols = slice(h * HD, (h + 1) * HD)
            scores = lax.dot_general(
                query_ref[r, :, cols], kv_ref[rows, cols], (((1,), (1,)), ((), ())), preferred_element_type=F32
            )
            scores = jnp.where(valid, scores, NEGATIVE_FILL)
            top = jnp.max(scores, axis=-1, keepdims=True)
            weights = jnp.exp2((scores - top) * EXP_SCALE)
            total = jnp.sum(weights, axis=-1, keepdims=True)
            acc = jnp.dot(
                weights.astype(BF16), kv_ref[rows, HEADW + h * HD : HEADW + (h + 1) * HD], preferred_element_type=F32
            )
            out_ref[r, :, cols] = (acc / total).astype(BF16)
            columns.append(top * SCALE + jnp.log(total))
        lse_ref[r] = columns_to_rows(columns)


def attend_tree(queries, new_kv, reachable):
    return pl.pallas_call(
        tree_kernel,
        out_shape=(
            jax.ShapeDtypeStruct((REQ_X, QROWS, HEADW), BF16),
            jax.ShapeDtypeStruct((REQ_X, KVH, QROWS), F32),
        ),
        cost_estimate=pl.CostEstimate(flops=10**9, bytes_accessed=10**6, transcendentals=10**5),
        name="attend_tree",
    )(queries, new_kv, reachable)


def mix_kernel(slots_ref, home_ref, home_lse_ref, tree_ref, tree_lse_ref, out_ref, mixed_ref):
    holders = home_ref.shape[0]
    for r in range(REQ_X):
        lses = [home_lse_ref[p, r] for p in range(holders)] + [tree_lse_ref[r]]
        top = lses[0]
        for lse in lses[1:]:
            top = jnp.maximum(top, lse)
        raised = [jnp.exp(lse - top) for lse in lses]
        total = raised[0]
        for one in raised[1:]:
            total = total + one
        shares = jnp.concatenate(raised + [total] * (HD // KVH - holders - 1), axis=0).T
        for h in range(KVH):
            cols = slice(h * HD, (h + 1) * HD)
            mixed = tree_ref[r, :, cols].astype(F32) * shares[:, holders * KVH + h : holders * KVH + h + 1]
            for p in range(holders):
                share = shares[:, p * KVH + h : p * KVH + h + 1]
                mixed = mixed + jnp.where(share > 0.0, home_ref[p, r, :, cols].astype(F32) * share, 0.0)
            whole_sum = shares[:, (holders + 1) * KVH + h : (holders + 1) * KVH + h + 1]
            mixed = (mixed / whole_sum).astype(BF16)
            for t in range(TOPK):
                start = t * ROWS + r * DRAFT
                mixed_ref[start : start + DRAFT, cols] = mixed[t * DRAFT : (t + 1) * DRAFT]
    buf_i = lax.broadcasted_iota(jnp.int32, (ROWS, BUF), 1)
    placed = None
    for t in range(TOPK):
        pick = (buf_i == slots_ref[:, t : t + 1]).astype(F32).astype(BF16)
        part = lax.dot_general(
            pick, mixed_ref[t * ROWS : (t + 1) * ROWS, :], (((0,), (0,)), ((), ())), preferred_element_type=F32
        )
        placed = part if placed is None else placed + part
    out_ref[...] = placed.astype(BF16)


def mix(slots, home_out, home_lse, tree_out, tree_lse):
    return pl.pallas_call(
        mix_kernel,
        out_shape=jax.ShapeDtypeStruct((BUF, HEADW), BF16),
        scratch_shapes=[VMEM((TOPK * ROWS, HEADW), BF16)],
        name="mix",
    )(slots, home_out, home_lse, tree_out, tree_lse)


def expert_out_kernel(parity_ref, mine_ref, theirs_ref, own_ref, other_ref, out_ref):
    total = jnp.dot(mine_ref[...], own_ref[...], preferred_element_type=F32)
    total = total + jnp.dot(theirs_ref[...], other_ref[...], preferred_element_type=F32)
    out_ref[...] = total.astype(BF16)


def expert_out(parity, rows, w_own, w_other):
    depth = w_own.shape[0]
    tile = 512
    return pl.pallas_call(
        expert_out_kernel,
        out_shape=jax.ShapeDtypeStruct((BUF, D), BF16),
        grid_spec=pltpu.PrefetchScalarGridSpec(
            num_scalar_prefetch=1,
            grid=(D // tile,),
            in_specs=[
                pl.BlockSpec((BUF, depth), lambda n, par: (0, par[0])),
                pl.BlockSpec((BUF, depth), lambda n, par: (0, 1 - par[0])),
                pl.BlockSpec((depth, tile), lambda n, par: (0, n)),
                pl.BlockSpec((depth, tile), lambda n, par: (0, n)),
            ],
            out_specs=pl.BlockSpec((BUF, tile), lambda n, par: (0, n)),
        ),
        name="expert_out",
    )(parity, rows, rows, w_own, w_other)


def combine_kernel(slots_ref, gates_ref, back_ref, out_ref):
    buf_i = lax.broadcasted_iota(jnp.int32, (ROWS, BUF), 1)
    total = None
    for t in range(TOPK):
        pick = (buf_i == slots_ref[:, t : t + 1]).astype(F32).astype(BF16)
        part = jnp.dot(pick, back_ref[...], preferred_element_type=F32) * gates_ref[:, t : t + 1]
        total = part if total is None else total + part
    out_ref[...] = total.astype(BF16)


def combine(slots, gates, back):
    tile = 512
    return pl.pallas_call(
        combine_kernel,
        out_shape=jax.ShapeDtypeStruct((ROWS, D), BF16),
        grid=(D // tile,),
        in_specs=[whole((ROWS, TOPK)), whole((ROWS, TOPK)), pl.BlockSpec((BUF, tile), lambda n: (0, n))],
        out_specs=pl.BlockSpec((ROWS, tile), lambda n: (0, n)),
        name="combine",
    )(slots, gates, back)


def ancestry(parent_ids):
    count_tokens = parent_ids.shape[-1]
    index_row = jnp.arange(count_tokens, dtype=jnp.int32)
    linked = (parent_ids[..., :, None] == index_row) & (index_row[:, None] > 0)
    reachable = (linked | (index_row[:, None] == index_row)).astype(BF16)
    for doubling in range(count_tokens.bit_length() - 1):
        reachable = jnp.minimum(jnp.matmul(reachable, reachable, preferred_element_type=F32), 1.0).astype(BF16)
    return reachable.astype(F32)


def partner_half(weight):
    count = lax.axis_size("req")
    rows = weight.shape[0] // count
    piece = lax.dynamic_slice_in_dim(weight, lax.axis_index("req") * rows, rows)
    piece = lax.ppermute(piece, "exp", [(i, i ^ 1) for i in range(lax.axis_size("exp"))])
    return lax.all_gather(piece, "req", axis=0, tiled=True)


def exchange(rows):
    return lax.all_to_all(rows, "exp", split_axis=0, concat_axis=0, tiled=True)


def body(
    hidden_in,
    router_choice,
    w_router,
    w_kv,
    w_query,
    w_out,
    kv_cache,
    page_count,
    tail_len,
    page_perm,
    parents,
    accepted_leaf,
):
    holder_count = lax.axis_size("req")
    owner_index = lax.axis_index("req")
    parity = (lax.axis_index("exp") % 2).astype(jnp.int32).reshape(1)
    group_requests = page_count.shape[1]
    pool_size = page_perm.shape[1]

    query_other = partner_half(w_query[0])
    out_other = partner_half(w_out[0])

    choice = router_choice.reshape(ROWS, TOPK)
    routed, normed, gates, slots = prologue(hidden_in.reshape(ROWS, D), choice, w_router)
    arrived = exchange(routed)
    query_back = exchange(expert_query(parity, arrived, w_query[0], query_other))

    reachable = ancestry(parents[0])
    depth_of = (jnp.sum(reachable, axis=-1) - 1.0).astype(jnp.int32)
    counts_all = page_count[0]
    lengths_all = (counts_all - 1) * PAGE + tail_len[0]
    own_lengths = lax.dynamic_slice_in_dim(lengths_all, owner_index * REQ_X, REQ_X)
    positions = (own_lengths[:, None] + depth_of).reshape(ROWS)
    half = HD // 2
    inverse_freq = 10000.0 ** (-jnp.arange(half, dtype=F32) / half)
    angles = positions.astype(F32)[:, None] * inverse_freq
    cosine, sine = jnp.cos(angles), jnp.sin(angles)
    cos_full = jnp.concatenate([cosine, cosine], axis=-1)
    sin_full = jnp.concatenate([-sine, sine], axis=-1)
    new_kv = project_kv(normed, w_kv, cos_full, sin_full)

    queries = pick_rotate(slots, cos_full, sin_full, query_back)
    shared = lax.all_gather(queries, "req", axis=0, tiled=True)

    ends = jnp.cumsum(counts_all)
    starts = ends - counts_all
    mine = owner_index * SLOTS + jnp.arange(SLOTS, dtype=jnp.int32)
    found = page_perm[0][None, :] == mine[:, None]
    page_pos = jnp.sum(jnp.where(found, jnp.arange(pool_size, dtype=jnp.int32)[None, :], 0), axis=1)
    slot_rank = jnp.sum((page_pos[None, :] < page_pos[:, None]).astype(jnp.int32), axis=1)
    slot_i = jnp.arange(SLOTS, dtype=jnp.int32)
    sorted_hot = slot_rank[None, :] == slot_i[:, None]
    order = jnp.sum(jnp.where(sorted_hot, slot_i[None, :], 0), axis=1)
    sorted_pos = jnp.sum(jnp.where(sorted_hot, page_pos[None, :], 0), axis=1)
    sorted_request = jnp.sum((ends[None, :] <= sorted_pos[:, None]).astype(jnp.int32), axis=1)
    member = sorted_request[:, None] == jnp.arange(group_requests, dtype=jnp.int32)[None, :]
    remaining = jnp.sum(jnp.where(member, (lengths_all + starts * PAGE)[None, :], 0), axis=1)
    sorted_valid = remaining - sorted_pos * PAGE

    held_out, held_lse = attend_pages(order, sorted_request, sorted_valid, shared, kv_cache[0])
    home_out = lax.all_to_all(
        held_out.reshape(holder_count, REQ_X, QROWS, HEADW), "req", split_axis=0, concat_axis=0, tiled=True
    )
    home_lse = lax.all_to_all(
        held_lse.reshape(holder_count, REQ_X, KVH, QROWS), "req", split_axis=0, concat_axis=0, tiled=True
    )
    tree_out, tree_lse = attend_tree(queries, new_kv, reachable)
    placed = mix(slots, home_out, home_lse, tree_out, tree_lse)
    out_back = exchange(expert_out(parity, exchange(placed), w_out[0], out_other))
    attn_out = combine(slots, gates, out_back).reshape(1, REQ_X, DRAFT, D)

    token_i = jnp.arange(DRAFT, dtype=jnp.int32)
    leaf_hot = accepted_leaf[0][:, None] == token_i[None, :]
    leaf_row = jnp.sum(jnp.where(leaf_hot[:, :, None], reachable, 0.0), axis=1)
    selector = (leaf_row[:, None, :] * (depth_of[:, None, :] == token_i[:, None]).astype(F32)).astype(BF16)
    cache_rows = jnp.einsum(
        "rdj,rjc->rdc", selector, new_kv.reshape(REQ_X, DRAFT, 2 * HEADW), preferred_element_type=F32
    ).astype(BF16)[None]
    return (attn_out, cache_rows)


def solution(mesh):
    placed = (
        P("exp", "req", None, None),
        P("exp", "req", None, None),
        P(),
        P(),
        P("exp", None, None),
        P("exp", None, None),
        P("exp", "req", None, None),
        P("exp", None),
        P("exp", None),
        P("exp", None),
        P("exp", "req", None),
        P("exp", "req"),
    )
    return jax.shard_map(
        body,
        mesh=mesh,
        in_specs=placed,
        out_specs=(P("exp", "req", None, None), P("exp", "req", None, None)),
        check_vma=False,
    )
```

time: 410 us -> 308 us (0.75); the launches traced: 402 us -> 307 us
  Pallas kernels: 0 us -> 86.7 us
  local copies, waits for them, and re-layouts: 96.2 us -> 11 us
  matrix products: 75.3 us -> 2.68 us
  other arithmetic: 72.5 us -> 3.34 us
  waiting for transfers between devices: 99.4 us -> 151 us
  blocking collectives: 17.4 us -> 9.57 us
    pallas_call x0 -> x9, Pallas kernels: none -> 86.7 us  [the longest x1 46.7 us: attend_pages(): pl.pallas_call(page_kernel, out_shape=(jax.ShapeDtypeStruct((count, QROWS...]
    dot_general x22 -> x4, matrix products: 75.3 us -> 2.68 us  [the longest x3 1.6 us: ancestry(): jnp.matmul(reachable, reachable, preferred_element_type=F32)]
    reduce_sum x13 -> x4, other arithmetic: 52.6 us -> 1.21 us  [the longest x1 0.66 us: body(): sorted_pos = jnp.sum(jnp.where(sorted_hot, page_pos[None, :], 0), axis=1)]
    all_gather x1 -> x3, waiting for transfers between devices: 0.02 us -> 29.2 us  [the longest x1 29.2 us: body(): shared = lax.all_gather(queries, 'req', axis=0, tiled=True)]
    dot_general x2 -> x0, local copies, waits for them, and re-layouts: 15 us -> none  [the longest x1 12.4 us: body(): jnp.dot(normed, w_kv, preferred_element_type=jnp.float32)]
    gather x11 -> x0, local copies, waits for them, and re-layouts: 14.9 us -> none  [the longest x2 11.3 us: body(): jnp.take(shared, slot_request, axis=0).reshape(SLOTS, query_rows, KVH, HD)]
    ppermute x0 -> x2, waiting for transfers between devices: none -> 13.8 us  [partner_half(): lax.ppermute(piece, 'exp', [(i, i ^ 1) for i in range(lax.axis_size('exp'...]
    convert_element_type x7 -> x1, local copies, waits for them, and re-layouts: 13.2 us -> 0.08 us  [body(): angles = positions.astype(F32)[:, None] * inverse_freq]
  transfers between devices with their start and end apart: 6 -> 10, of which waited for: 4 -> 8; matrix products, arithmetic and copies ran while one was open for 29% -> 3% of each run, Pallas kernels for 0% -> 7%
where the time goes in v1:
time: 308 us; the launch traced here: 307 us
  waiting for transfers between devices  151 us (49%)
  Pallas kernels  86.7 us (28%)
  starting transfers between devices  29 us (9%)
  between operations  13.9 us (5%)
  local copies, waits for them, and re-layouts  11 us (4%)
  blocking collectives  9.57 us (3%)
  other arithmetic  3.34 us (1%)
    all_to_all x4, waiting for transfers between devices, exchange(): return lax.all_to_all(rows, 'exp', split_axis=0, concat_axis=0, tiled=True)  68.9 us
    pallas_call x1, Pallas kernels, attend_pages(): pl.pallas_call(page_kernel, out_shape=(jax.ShapeDtypeStruct((count, QROWS...  46.7 us
    all_to_all x1, waiting for transfers between devices, body(): lax.all_to_all(held_out.reshape(holder_count, REQ_X, QROWS, HEADW), 'req'...  38.5 us
    all_gather x1, waiting for transfers between devices, body(): shared = lax.all_gather(queries, 'req', axis=0, tiled=True)  29.2 us
    all_to_all x4, starting transfers between devices, exchange(): return lax.all_to_all(rows, 'exp', split_axis=0, concat_axis=0, tiled=True)  21.4 us
    ppermute x2, waiting for transfers between devices, partner_half(): lax.ppermute(piece, 'exp', [(i, i ^ 1) for i in range(lax.axis_size('exp'...  13.8 us
    all_to_all x1, blocking collectives, body(): lax.all_to_all(held_lse.reshape(holder_count, REQ_X, KVH, QROWS), 'req',...  9.57 us
    pallas_call x1, Pallas kernels, mix(): pl.pallas_call(mix_kernel, out_shape=jax.ShapeDtypeStruct((BUF, HEADW), B...  9.42 us
  transfers between devices with their start and end apart: 10, of which 8 were waited for; matrix products, arithmetic and copies ran while one was open for 3% of the time, Pallas kernels for 7%

profile of v1, /device:TPU:0, one launch (start us, length us, event | category | flops | bytes accessed | tf_op | source)
XLA Modules:
  0.0 306.8 jit_solution(12631120973309006248)
XLA Ops:
  9.8 6.3 %collective-permute-done = bf16[256,512]{1,0:T(8,128)(2,1)S(1)} collective-permute-done((bf16[256,512]{1,0:T(8,128)(2,1)S(1)}, bf16[256,512]{1,0:T(8,128)(2,1)S(1)}, u32[]{:S(2)}, u32[]{:S(2)}) %collective-permute-start) | collective-permute-done | bytes 262176 | tf_op jit(solution)/shard_map/ppermute | solution.py:404
  18.4 1.8 copy.28.router_ref
  20.2 3.5 %prologue.1 = (bf16[384,2048]{1,0:T(8,128)(2,1)}, bf16[128,2048]{1,0:T(8,128)(2,1)}, f32[128,2]{1,0:T(8,128)}, s32[128,2]{1,0:T(8,128)}) custom-call(bf16[128,2048]{1,0:T(8,128)(2,1)} %bitcast.62, s32[128,2]{1,0:T(8,128)} %copy.27.choice_ref, s32[2,128]{1,0:T(2,128)} %bitcast.64, bf16[2048,8]{1,0:T(8,128)(2,1)} %copy.28.router_ref), custom_call_target="tpu_custom_call" | custom-call | tf_op jit(solution)/shard_map/prologue/pallas_call | solution.py:80
  23.7 7.3 %all-to-all-start = ((bf16[16,24,2048]{2,1,0:T(8,128)(2,1)}), bf16[16,24,2048]{2,1,0:T(8,128)(2,1)S(1)}, u32[]{:S(2)}, u32[]{:S(2)}) async-start(bf16[16,24,2048]{2,1,0:T(8,128)(2,1)} %bitcast.60), calls=%async_computation | async-start | bytes 3145728 | tf_op jit(solution)/shard_map/all_to_all | solution.py:409
  33.0 20.8 %all-to-all-done = bf16[16,24,2048]{2,1,0:T(8,128)(2,1)S(1)} async-done(((bf16[16,24,2048]{2,1,0:T(8,128)(2,1)}), bf16[16,24,2048]{2,1,0:T(8,128)(2,1)S(1)}, u32[]{:S(2)}, u32[]{:S(2)}) %all-to-all-start) | async-done | bytes 1572896 | tf_op jit(solution)/shard_map/all_to_all | solution.py:409
  54.9 5.8 %expert_query.1 = bf16[384,1024]{1,0:T(8,128)(2,1)} custom-call(s32[1]{0:T(128)} %bitcast.2.parity_ref, bf16[384,2048]{1,0:T(8,128)(2,1)} %bitcast.51, bf16[2048,512]{1,0:T(8,128)(2,1)} %bitcast.57, bf16[2048,512]{1,0:T(8,128)(2,1)} %all-gather.4.cloned.1.call-done.other_ref), custom_call_target="tpu_custom_call" | custom-call | tf_op jit(solution)/shard_map/expert_query/pallas_call | solution.py:106
  60.7 3.7 %all-to-all-start.1 = ((bf16[16,24,1024]{2,1,0:T(8,128)(2,1)}), bf16[16,24,1024]{2,1,0:T(8,128)(2,1)S(1)}, u32[]{:S(2)}, u32[]{:S(2)}) async-start(bf16[16,24,1024]{2,1,0:T(8,128)(2,1)} %bitcast.55), calls=%async_computation.1 | async-start | bytes 1572864 | tf_op jit(solution)/shard_map/all_to_all | solution.py:409
  65.9 12.4 %all-to-all-done.1 = bf16[16,24,1024]{2,1,0:T(8,128)(2,1)S(1)} async-done(((bf16[16,24,1024]{2,1,0:T(8,128)(2,1)}), bf16[16,24,1024]{2,1,0:T(8,128)(2,1)S(1)}, u32[]{:S(2)}, u32[]{:S(2)}) %all-to-all-start.1) | async-done | bytes 786464 | tf_op jit(solution)/shard_map/all_to_all | solution.py:409
  79.2 2.8 pick_rotate.1.query_ref
  83.9 29.2 %all-gather.6.cloned.1.call-done.query_ref = bf16[16,128,1024]{2,1,0:T(8,128)(2,1)} async-done(((bf16[2,128,1024]{2,1,0:T(8,128)(2,1)}), bf16[16,128,1024]{2,1,0:T(8,128)(2,1)}) %all-gather.6.cloned.1.call-update) | async-done | bytes 4194320 | tf_op jit(solution)/shard_map/all_gather | solution.py:455
  113.1 46.7 %attend_pages.1 = (bf16[16,128,1024]{2,1,0:T(8,128)(2,1)}, f32[16,8,128]{2,1,0:T(8,128)}) custom-call(s32[16]{0:T(128)} %get-tuple-element.21.order_ref, s32[16]{0:T(128)} %copy-done.9, s32[16]{0:T(128)} %multiply_subtract_fusion.valid_ref, bf16[16,128,1024]{2,1,0:T(8,128)(2,1)} %all-gather.6.cloned.1.call-done.query_ref, bf16[16,128,2048]{2,1,0:T(8,128)(2,1)} %bitcast.47), custom_call_target="tpu_custom_call" | custom-call | tf_op jit(solution)/shard_map/attend_pages/pallas_call | solution.py:240
  159.8 9.6 %all_to_all.54.home_lse_ref = f32[8,2,8,128]{3,2,1,0:T(8,128)} all-to-all(f32[8,2,8,128]{3,2,1,0:T(8,128)} %bitcast.63), channel_id=1, replica_groups=mesh['req'=8,'exp'=16] {'req'}, dimensions={0} | all-to-all | bytes 131072 | tf_op jit(solution)/shard_map/all_to_all | solution.py:476
  169.4 4.5 %all-to-all-start.2 = ((bf16[8,2,128,1024]{3,2,1,0:T(8,128)(2,1)}), bf16[8,2,128,1024]{3,2,1,0:T(8,128)(2,1)}, u32[]{:S(2)}, u32[]{:S(2)}) async-start(bf16[8,2,128,1024]{3,2,1,0:T(8,128)(2,1)} %bitcast.53), calls=%async_computation.2 | async-start | bytes 8388608 | tf_op jit(solution)/shard_map/all_to_all | solution.py:473
  176.2 7.5 %collective-permute-done.1 = bf16[64,2048]{1,0:T(8,128)(2,1)S(1)} collective-permute-done((bf16[64,2048]{1,0:T(8,128)(2,1)S(1)}, bf16[64,2048]{1,0:T(8,128)(2,1)S(1)}, u32[]{:S(2)}, u32[]{:S(2)}) %collective-permute-start.1) | collective-permute-done | bytes 262176 | tf_op jit(solution)/shard_map/ppermute | solution.py:404
  184.5 6.0 %project_kv.1.kv_ref = bf16[128,2048]{1,0:T(8,128)(2,1)} custom-call(bf16[128,2048]{1,0:T(8,128)(2,1)} %get-tuple-element.15.normed_ref, bf16[2048,2048]{1,0:T(8,128)(2,1)} %weight_ref.1, f32[128,128]{1,0:T(8,128)} %get-tuple-element.28.cos_ref, f32[128,128]{1,0:T(8,128)} %get-tuple-element.29.sin_ref), custom_call_target="tpu_custom_call" | custom-call | flops 1073741824 | bytes 8388608 | tf_op jit(solution)/shard_map/project_kv/pallas_call | solution.py:164
  190.5 3.0 attend_tree.1
  193.5 38.5 %all-to-all-done.2.home_ref = bf16[8,2,128,1024]{3,2,1,0:T(8,128)(2,1)} async-done(((bf16[8,2,128,1024]{3,2,1,0:T(8,128)(2,1)}), bf16[8,2,128,1024]{3,2,1,0:T(8,128)(2,1)}, u32[]{:S(2)}, u32[]{:S(2)}) %all-to-all-start.2) | async-done | bytes 4194336 | tf_op jit(solution)/shard_map/all_to_all | solution.py:473
  232.0 9.4 %mix.1 = bf16[384,1024]{1,0:T(8,128)(2,1)} custom-call(s32[128,2]{1,0:T(8,128)} %get-tuple-element.10.slots_ref, bf16[8,2,128,1024]{3,2,1,0:T(8,128)(2,1)} %all-to-all-done.2.home_ref, f32[8,2,8,128]{3,2,1,0:T(8,128)} %all_to_all.54.home_lse_ref, bf16[2,128,1024]{2,1,0:T(8,128)(2,1)} %get-tuple-element.16.tree_ref, f32[2,8,128]{2,1,0:T(8,128)} %get-tuple-element.17.tree_lse_ref), custom_call_target="tpu_custom_call" | custom-call | tf_op jit(solution)/shard_map/mix/pallas_call | solution.py:333
  241.4 6.5 %all-to-all-start.4 = ((bf16[16,24,1024]{2,1,0:T(8,128)(2,1)}), bf16[16,24,1024]{2,1,0:T(8,128)(2,1)S(1)}, u32[]{:S(2)}, u32[]{:S(2)}) async-start(bf16[16,24,1024]{2,1,0:T(8,128)(2,1)} %bitcast.56), calls=%async_computation.4 | async-start | bytes 1572864 | tf_op jit(solution)/shard_map/all_to_all | solution.py:409
  248.0 14.2 %all-to-all-done.4 = bf16[16,24,1024]{2,1,0:T(8,128)(2,1)S(1)} async-done(((bf16[16,24,1024]{2,1,0:T(8,128)(2,1)}), bf16[16,24,1024]{2,1,0:T(8,128)(2,1)S(1)}, u32[]{:S(2)}, u32[]{:S(2)}) %all-to-all-start.4) | async-done | bytes 786464 | tf_op jit(solution)/shard_map/all_to_all | solution.py:409
  263.1 5.5 %expert_out.1 = bf16[384,2048]{1,0:T(8,128)(2,1)} custom-call(s32[1]{0:T(128)} %bitcast.2.parity_ref, bf16[384,1024]{1,0:T(8,128)(2,1)} %bitcast.48, bf16[384,1024]{1,0:T(8,128)(2,1)} %bitcast.49, bf16[512,2048]{1,0:T(8,128)(2,1)} %bitcast.58, bf16[512,2048]{1,0:T(8,128)(2,1)} %all-gather.8.cloned.1.call-done.other_ref), custom_call_target="tpu_custom_call" | custom-call | tf_op jit(solution)/shard_map/expert_out/pallas_call | solution.py:350
  268.5 3.8 %all-to-all-start.5 = ((bf16[16,24,2048]{2,1,0:T(8,128)(2,1)}), bf16[16,24,2048]{2,1,0:T(8,128)(2,1)S(1)}, u32[]{:S(2)}, u32[]{:S(2)}) async-start(bf16[16,24,2048]{2,1,0:T(8,128)(2,1)} %bitcast.52), calls=%async_computation.5 | async-start | bytes 3145728 | tf_op jit(solution)/shard_map/all_to_all | solution.py:409
  273.5 21.6 %all-to-all-done.5 = bf16[16,24,2048]{2,1,0:T(8,128)(2,1)S(1)} async-done(((bf16[16,24,2048]{2,1,0:T(8,128)(2,1)}), bf16[16,24,2048]{2,1,0:T(8,128)(2,1)S(1)}, u32[]{:S(2)}, u32[]{:S(2)}) %all-to-all-start.5) | async-done | bytes 1572896 | tf_op jit(solution)/shard_map/all_to_all | solution.py:409
  296.2 4.0 %combine.1 = bf16[128,2048]{1,0:T(8,128)(2,1)} custom-call(s32[128,2]{1,0:T(8,128)} %get-tuple-element.10.slots_ref, f32[128,2]{1,0:T(8,128)} %get-tuple-element.11.gates_ref, bf16[384,2048]{1,0:T(8,128)(2,1)} %bitcast.50), custom_call_target="tpu_custom_call" | custom-call | tf_op jit(solution)/shard_map/combine/pallas_call | solution.py:380
  (68 shorter events, 18.4 us)
Async XLA Ops:
  7.2 46.6 %all-gather.4.cloned.1.call-start = ((), (), s32[]{:S(2)}) async-start(), calls=%async_computation.6 | async-start | bytes 2359296 | tf_op jit(solution)/shard_map/all_gather | solution.py:405
  8.2 8.0 %collective-permute-start = (bf16[256,512]{1,0:T(8,128)(2,1)S(1)}, bf16[256,512]{1,0:T(8,128)(2,1)S(1)}, u32[]{:S(2)}, u32[]{:S(2)}) collective-permute-start(bf16[256,512]{1,0:T(8,128)(2,1)S(1)} %dynamic-slice_bitcast_fusion.1), channel_id=1, source_target_pairs={{0,1},{1,0},{2,3},{3,2},{4,5},{5,4},{6,7},{7,6},{8,9},{9,8},{10,11... | collective-permute-start | bytes 786440 | tf_op jit(solution)/shard_map/ppermute | solution.py:404
  16.1 0.7 copy-start.5
  17.7 2.5 copy-start.7
  20.2 10.8 %copy-start.8 = (s32[1,16]{1,0:T(1,128)S(1)}, s32[1,16]{1,0:T(1,128)}, u32[]{:S(2)}) copy-start(s32[1,16]{1,0:T(1,128)} %param.19) | copy-start | bytes 196
  20.2 11.1 %copy-start.12 = (s32[1,2]{1,0:T(1,128)S(1)}, s32[1,2]{1,0:T(1,128)}, u32[]{:S(2)}) copy-start(s32[1,2]{1,0:T(1,128)} %param.23) | copy-start | bytes 28
  20.2 11.2 %copy-start.10 = (s32[1,16]{1,0:T(1,128)S(1)}, s32[1,16]{1,0:T(1,128)}, u32[]{:S(2)}) copy-start(s32[1,16]{1,0:T(1,128)} %param.20) | copy-start | bytes 196
  20.2 11.2 %copy-start.11 = (s32[1,2,64]{2,1,0:T(2,128)S(1)}, s32[1,2,64]{2,1,0:T(2,128)}, u32[]{:S(2)}) copy-start(s32[1,2,64]{2,1,0:T(2,128)} %param.22) | copy-start | bytes 1540
  23.7 30.0 %all-to-all-start = ((bf16[16,24,2048]{2,1,0:T(8,128)(2,1)}), bf16[16,24,2048]{2,1,0:T(8,128)(2,1)S(1)}, u32[]{:S(2)}, u32[]{:S(2)}) async-start(bf16[16,24,2048]{2,1,0:T(8,128)(2,1)} %bitcast.60), calls=%async_computation | async-start | bytes 3145728 | tf_op jit(solution)/shard_map/all_to_all | solution.py:409
  53.7 1.2 copy-start.2
  60.7 21.3 %copy-start.13 = (s32[1,128]{1,0:T(1,128)S(1)}, s32[1,128]{1,0:T(1,128)}, u32[]{:S(2)}) copy-start(s32[1,128]{1,0:T(1,128)} %param.21) | copy-start | bytes 1540
  60.7 17.5 %all-to-all-start.1 = ((bf16[16,24,1024]{2,1,0:T(8,128)(2,1)}), bf16[16,24,1024]{2,1,0:T(8,128)(2,1)S(1)}, u32[]{:S(2)}, u32[]{:S(2)}) async-start(bf16[16,24,1024]{2,1,0:T(8,128)(2,1)} %bitcast.55), calls=%async_computation.1 | async-start | bytes 1572864 | tf_op jit(solution)/shard_map/all_to_all | solution.py:409
  64.5 48.7 %all-gather.6.cloned.1.call-start = ((), (), s32[]{:S(2)}) async-start(), calls=%async_computation.7 | async-start | bytes 4718592 | tf_op jit(solution)/shard_map/all_gather | solution.py:455
  78.3 0.9 copy-start.3
  83.2 29.9 %copy-start.9 = (s32[16]{0:T(128)}, s32[16]{0:T(128)S(1)}, u32[]{:S(2)}) copy-start(s32[16]{0:T(128)S(1)} %convert_reduce_fusion.request_ref) | copy-start | bytes 196
  169.4 62.6 %all-to-all-start.2 = ((bf16[8,2,128,1024]{3,2,1,0:T(8,128)(2,1)}), bf16[8,2,128,1024]{3,2,1,0:T(8,128)(2,1)}, u32[]{:S(2)}, u32[]{:S(2)}) async-start(bf16[8,2,128,1024]{3,2,1,0:T(8,128)(2,1)} %bitcast.53), calls=%async_computation.2 | async-start | bytes 8388608 | tf_op jit(solution)/shard_map/all_to_all | solution.py:473
  173.9 74.1 %all-gather.8.cloned.1.call-start = ((), (), s32[]{:S(2)}) async-start(), calls=%async_computation.8 | async-start | bytes 2359296 | tf_op jit(solution)/shard_map/all_gather | solution.py:405
  175.0 8.8 %collective-permute-start.1 = (bf16[64,2048]{1,0:T(8,128)(2,1)S(1)}, bf16[64,2048]{1,0:T(8,128)(2,1)S(1)}, u32[]{:S(2)}, u32[]{:S(2)}) collective-permute-start(bf16[64,2048]{1,0:T(8,128)(2,1)S(1)} %dynamic-slice_bitcast_fusion), channel_id=1, source_target_pairs={{0,1},{1,0},{2,3},{3,2},{4,5},{5,4},{6,7},{7,6},{8,9},{9,8},{10,11... | collective-permute-start | bytes 786440 | tf_op jit(solution)/shard_map/ppermute | solution.py:404
  183.7 0.7 copy-start.6
  241.4 20.7 %all-to-all-start.4 = ((bf16[16,24,1024]{2,1,0:T(8,128)(2,1)}), bf16[16,24,1024]{2,1,0:T(8,128)(2,1)S(1)}, u32[]{:S(2)}, u32[]{:S(2)}) async-start(bf16[16,24,1024]{2,1,0:T(8,128)(2,1)} %bitcast.56), calls=%async_computation.4 | async-start | bytes 1572864 | tf_op jit(solution)/shard_map/all_to_all | solution.py:409
  262.2 0.9 copy-start
  268.5 3.9 %copy-start.4 = (bf16[128,2048]{1,0:T(8,128)(2,1)S(1)}, bf16[128,2048]{1,0:T(8,128)(2,1)}, u32[]{:S(2)}) copy-start(bf16[128,2048]{1,0:T(8,128)(2,1)} %project_kv.1.kv_ref) | copy-start | bytes 1572868
  268.5 26.5 %all-to-all-start.5 = ((bf16[16,24,2048]{2,1,0:T(8,128)(2,1)}), bf16[16,24,2048]{2,1,0:T(8,128)(2,1)S(1)}, u32[]{:S(2)}, u32[]{:S(2)}) async-start(bf16[16,24,2048]{2,1,0:T(8,128)(2,1)} %bitcast.52), calls=%async_computation.5 | async-start | bytes 3145728 | tf_op jit(solution)/shard_map/all_to_all | solution.py:409
  295.1 1.2 copy-start.1
Sparse Core Ops, SparseCore 0:
  17.0 28.0 all-gather.3
  82.1 31.0 all-gather.5
  184.6 36.5 all-gather.7

commit v2 on v1

--- a/solution.py
+++ b/solution.py
@@ -28,6 +28,9 @@
 F32 = jnp.float32
 BF16 = jnp.bfloat16
 VMEM = pltpu.VMEM
+DMA = pltpu.SemaphoreType.DMA
+MESH = pl.DeviceIdType.MESH
+ABSENT = -1e29
 
 
 def whole(shape):
@@ -38,7 +41,7 @@
     return x * cos_full + pltpu.roll(x, HD // 2, 1) * sin_full
 
 
-def prologue_kernel(hidden_ref, choice_ref, choice_t_ref, router_ref, routed_ref, normed_ref, gates_ref, slots_ref):
+def prologue_kernel(hidden_ref, choice_ref, choice_t_ref, router_ref, routed_ref, normed_ref, gates_ref, slots_ref, slot_rows_ref):
     tokens = hidden_ref[...].astype(F32)
     mean_sq = jnp.mean(tokens * tokens, axis=-1, keepdims=True)
     normed = (tokens * lax.rsqrt(mean_sq + NORM_EPSILON)).astype(BF16)
@@ -69,6 +72,9 @@
         + jnp.sum(jnp.where(hot_t[t], before_t, 0.0), axis=0, keepdims=True).astype(jnp.int32)
         for t in range(TOPK)
     ]
+    for r in range(REQ_X):
+        lanes = slice(r * DRAFT, (r + 1) * DRAFT)
+        slot_rows_ref[r : r + 1, :] = jnp.concatenate([row[:, lanes] for row in slot_row], axis=1)
     buf_i = lax.broadcasted_iota(jnp.int32, (BUF, ROWS), 0)
     spread = ((buf_i == slot_row[0]) | (buf_i == slot_row[1])).astype(F32).astype(BF16)
     for n in range(D // 512):
@@ -84,6 +90,7 @@
             jax.ShapeDtypeStruct((ROWS, D), BF16),
             jax.ShapeDtypeStruct((ROWS, TOPK), F32),
             jax.ShapeDtypeStruct((ROWS, TOPK), jnp.int32),
+            jax.ShapeDtypeStruct((REQ_X, QROWS), jnp.int32),
         ),
         name="prologue",
     )(hidden, choice, choice.T, w_router)
@@ -177,12 +184,22 @@
     )(normed, w_kv, cos_full, sin_full)
 
 
-def columns_to_rows(columns):
-    lane = lax.broadcasted_iota(jnp.int32, (QROWS, HD), 1)
-    wide = jnp.zeros((QROWS, HD), F32)
-    for h, column in enumerate(columns):
-        wide = jnp.where(lane == h, column, wide)
-    return wide.T[:KVH]
+def block_attention(keys, values, queries, valid):
+    scores = lax.dot_general(keys, queries, (((1,), (1,)), ((), ())), preferred_element_type=F32)
+    scores = jnp.where(valid, scores, NEGATIVE_FILL)
+    top = jnp.max(scores, axis=0, keepdims=True)
+    weights = jnp.exp2((scores - top) * EXP_SCALE)
+    total = jnp.sum(weights, axis=0, keepdims=True)
+    acc = lax.dot_general(values, weights.astype(BF16), (((0,), (0,)), ((), ())), preferred_element_type=F32)
+    return top, total, acc
+
+
+def head_rows(h):
+    return slice(h * HD, (h + 1) * HD)
+
+
+def value_cols(h):
+    return slice(HEADW + h * HD, HEADW + (h + 1) * HD)
 
 
 def page_kernel(order_ref, request_ref, valid_ref, query_ref, cache_ref, out_ref, lse_ref, max_ref, sum_ref, acc_ref):
@@ -202,37 +219,26 @@
         sum_ref[...] = jnp.zeros_like(sum_ref)
         acc_ref[...] = jnp.zeros_like(acc_ref)
 
-    lane = lax.broadcasted_iota(jnp.int32, (QROWS, PAGE), 1)
-    valid = lane < valid_ref[i]
+    valid = lax.broadcasted_iota(jnp.int32, (PAGE, QROWS), 0) < valid_ref[i]
     for h in range(KVH):
-        cols = slice(h * HD, (h + 1) * HD)
-        scores = lax.dot_general(
-            query_ref[0, :, cols], cache_ref[0, :, cols], (((1,), (1,)), ((), ())), preferred_element_type=F32
+        rows = head_rows(h)
+        page_max, page_sum, page_acc = block_attention(
+            cache_ref[0, :, rows], cache_ref[0, :, value_cols(h)], query_ref[0, :, rows], valid
         )
-        scores = jnp.where(valid, scores, NEGATIVE_FILL)
-        page_max = jnp.max(scores, axis=-1, keepdims=True)
-        weights = jnp.exp2((scores - page_max) * EXP_SCALE)
-        page_sum = jnp.sum(weights, axis=-1, keepdims=True)
-        page_acc = jnp.dot(
-            weights.astype(BF16), cache_ref[0, :, HEADW + h * HD : HEADW + (h + 1) * HD], preferred_element_type=F32
-        )
-        old_max = max_ref[h]
+        old_max = max_ref[h : h + 1]
         new_max = jnp.maximum(old_max, page_max)
         old_scale = jnp.exp2((old_max - new_max) * EXP_SCALE)
         page_scale = jnp.exp2((page_max - new_max) * EXP_SCALE)
-        max_ref[h] = new_max
-        sum_ref[h] = sum_ref[h] * old_scale + page_sum * page_scale
-        acc_ref[:, cols] = acc_ref[:, cols] * old_scale + page_acc * page_scale
+        max_ref[h : h + 1] = new_max
+        sum_ref[h : h + 1] = sum_ref[h : h + 1] * old_scale + page_sum * page_scale
+        acc_ref[rows] = acc_ref[rows] * old_scale + page_acc * page_scale
 
     @pl.when(finishes)
     def _():
-        columns = []
+        total = sum_ref[...]
         for h in range(KVH):
-            cols = slice(h * HD, (h + 1) * HD)
-            total = sum_ref[h]
-            out_ref[0, :, cols] = (acc_ref[:, cols] / total).astype(BF16)
-            columns.append(max_ref[h] * SCALE + jnp.log(total))
-        lse_ref[here] = columns_to_rows(columns)
+            out_ref[0, head_rows(h)] = (acc_ref[head_rows(h)] / total[h : h + 1]).astype(BF16)
+        lse_ref[here] = max_ref[...] * SCALE + jnp.log(total)
 
 
 def attend_pages(order, requests, valid, queries, cache):
@@ -240,7 +246,7 @@
     return pl.pallas_call(
         page_kernel,
         out_shape=(
-            jax.ShapeDtypeStruct((count, QROWS, HEADW), BF16),
+            jax.ShapeDtypeStruct((count, HEADW, QROWS), BF16),
             jax.ShapeDtypeStruct((count, KVH, QROWS), F32),
         ),
         grid_spec=pltpu.PrefetchScalarGridSpec(
@@ -251,91 +257,175 @@
                 pl.BlockSpec((1, PAGE, 2 * HEADW), lambda i, o, r, v: (o[i], 0, 0)),
             ],
             out_specs=(
-                pl.BlockSpec((1, QROWS, HEADW), lambda i, o, r, v: (r[i], 0, 0)),
+                pl.BlockSpec((1, HEADW, QROWS), lambda i, o, r, v: (r[i], 0, 0)),
                 pl.BlockSpec((count, KVH, QROWS), lambda i, o, r, v: (0, 0, 0)),
             ),
-            scratch_shapes=[VMEM((KVH, QROWS, 1), F32), VMEM((KVH, QROWS, 1), F32), VMEM((QROWS, HEADW), F32)],
+            scratch_shapes=[VMEM((KVH, QROWS), F32), VMEM((KVH, QROWS), F32), VMEM((HEADW, QROWS), F32)],
         ),
         name="attend_pages",
     )(order, requests, valid, queries, cache)
 
 
-def tree_kernel(query_ref, kv_ref, reach_ref, out_ref, lse_ref):
+def shares_of(lses):
+    top = lses[0]
+    for lse in lses[1:]:
+        top = jnp.maximum(top, lse)
+    raised = [jnp.exp(lse - top) for lse in lses]
+    total = raised[0]
+    for one in raised[1:]:
+        total = total + one
+    return [one / total for one in raised], top + jnp.log(total)
+
+
+def merge_parts(parts, store):
+    shares, lse = shares_of([part[1] for part in parts])
+    for h in range(KVH):
+        rows = head_rows(h)
+        merged = None
+        for (ref, part_lse, raw), share in zip(parts, shares):
+            values = ref[rows].astype(F32)
+            if raw:
+                values = jnp.where(part_lse[h : h + 1] > ABSENT, values, 0.0)
+            values = values * share[h : h + 1]
+            merged = values if merged is None else merged + values
+        store(rows, merged.astype(BF16))
+    return lse
+
+
+def home_kernel(
+    out_ref, lse_ref, query_ref, kv_ref, reach_ref, slot_rows_ref, placed_ref,
+    sib_buf, sib_lse, send_buf, send_lse, recv_buf, recv_lse, tree_buf, mixed_buf,
+    sib_send, sib_recv, ring_send, ring_recv,
+):
+    me = lax.axis_index("req")
+    count = lax.axis_size("req")
+    chips = count // 2
+    core, chip = me % 2, me // 2
+    sibling = chip * 2 + 1 - core
+    after = ((chip + 1) % chips) * 2 + core
+    before = ((chip + chips - 1) % chips) * 2 + core
+    barrier = pltpu.get_barrier_semaphore()
+    for peer in (sibling, after, before):
+        pl.semaphore_signal(barrier, inc=1, device_id={"req": peer}, device_id_type=MESH)
+    pl.semaphore_wait(barrier, 3)
+
+    def copy(src, dst, send, recv, peer):
+        one = pltpu.make_async_remote_copy(
+            src_ref=src, dst_ref=dst, send_sem=send, recv_sem=recv, device_id={"req": peer}, device_id_type=MESH
+        )
+        one.start()
+        return one
+
+    owners = [(chip + off) % chips for off in (2, 1, 3, 0)]
+    mine = [(owner * 2 + core) * REQ_X for owner in owners]
+    sib_copies = []
+    for k, owner in enumerate(owners):
+        theirs = (owner * 2 + 1 - core) * REQ_X
+        sib_copies.append([
+            copy(lse_ref.at[pl.ds(theirs, REQ_X)], sib_lse.at[k], sib_send.at[2 * k], sib_recv.at[2 * k], sibling),
+            copy(out_ref.at[pl.ds(theirs, REQ_X)], sib_buf.at[k], sib_send.at[2 * k + 1], sib_recv.at[2 * k + 1], sibling),
+        ])
+
+    tree_lses = []
     for r in range(REQ_X):
-        rows = slice(r * DRAFT, (r + 1) * DRAFT)
-        reach = reach_ref[r]
-        valid = jnp.concatenate([reach] * TOPK, axis=0) > 0.5
-        columns = []
+        tokens = slice(r * DRAFT, (r + 1) * DRAFT)
+        valid = reach_ref[r] > 0.5
+        tops, totals = [], []
         for h in range(KVH):
-            cols = slice(h * HD, (h + 1) * HD)
-            scores = lax.dot_general(
-                query_ref[r, :, cols], kv_ref[rows, cols], (((1,), (1,)), ((), ())), preferred_element_type=F32
+            top, total, acc = block_attention(
+                kv_ref[tokens, head_rows(h)], kv_ref[tokens, value_cols(h)], query_ref[r, :, head_rows(h)], valid
             )
-            scores = jnp.where(valid, scores, NEGATIVE_FILL)
-            top = jnp.max(scores, axis=-1, keepdims=True)
-            weights = jnp.exp2((scores - top) * EXP_SCALE)
-            total = jnp.sum(weights, axis=-1, keepdims=True)
-            acc = jnp.dot(
-                weights.astype(BF16), kv_ref[rows, HEADW + h * HD : HEADW + (h + 1) * HD], preferred_element_type=F32
-            )
-            out_ref[r, :, cols] = (acc / total).astype(BF16)
-            columns.append(top * SCALE + jnp.log(total))
-        lse_ref[r] = columns_to_rows(columns)
-
-
-def attend_tree(queries, new_kv, reachable):
-    return pl.pallas_call(
-        tree_kernel,
-        out_shape=(
-            jax.ShapeDtypeStruct((REQ_X, QROWS, HEADW), BF16),
-            jax.ShapeDtypeStruct((REQ_X, KVH, QROWS), F32),
-        ),
-        cost_estimate=pl.CostEstimate(flops=10**9, bytes_accessed=10**6, transcendentals=10**5),
-        name="attend_tree",
-    )(queries, new_kv, reachable)
-
-
-def mix_kernel(slots_ref, home_ref, home_lse_ref, tree_ref, tree_lse_ref, out_ref, mixed_ref):
-    holders = home_ref.shape[0]
+            tree_buf[r, head_rows(h)] = (acc / total).astype(BF16)
+            tops.append(top)
+            totals.append(total)
+        tree_lses.append(jnp.concatenate(tops, axis=0) * SCALE + jnp.log(jnp.concatenate(totals, axis=0)))
+
+    def chip_parts(k, r):
+        return [
+            (out_ref.at[mine[k] + r], lse_ref[mine[k] + r], True),
+            (sib_buf.at[k, r], sib_lse[k, r], True),
+        ]
+
+    def relay(slot, parts, peer):
+        def store(rows, values):
+            send_buf[slot, rows] = values
+
+        send_lse[slot] = merge_parts(parts, store)
+        return [
+            copy(send_lse.at[slot], recv_lse.at[slot], ring_send.at[2 * slot], ring_recv.at[2 * slot], peer),
+            copy(send_buf.at[slot], recv_buf.at[slot], ring_send.at[2 * slot + 1], ring_recv.at[2 * slot + 1], peer),
+        ]
+
+    def arrive(copies):
+        for one in copies:
+            one.wait_recv()
+
+    def came(slot):
+        return (recv_buf.at[slot], recv_lse[slot], False)
+
+    ring = [None] * 6
+    arrive(sib_copies[0])
+    ring[0] = relay(0, chip_parts(0, 0), after)
+    ring[1] = relay(1, chip_parts(0, 1), before)
+    arrive(sib_copies[1])
+    ring[2] = relay(2, chip_parts(1, 1), after)
+    arrive(sib_copies[2])
+    ring[3] = relay(3, chip_parts(2, 0), before)
+    arrive(ring[0])
+    ring[4] = relay(4, chip_parts(1, 0) + [came(0)], after)
+    arrive(ring[1])
+    ring[5] = relay(5, chip_parts(2, 1) + [came(1)], before)
+    arrive(sib_copies[3])
+
+    buf_i = lax.broadcasted_iota(jnp.int32, (BUF, QROWS), 0)
+    total = None
+    for slot in (2, 3, 4, 5):
+        arrive(ring[slot])
     for r in range(REQ_X):
-        lses = [home_lse_ref[p, r] for p in range(holders)] + [tree_lse_ref[r]]
-        top = lses[0]
-        for lse in lses[1:]:
-            top = jnp.maximum(top, lse)
-        raised = [jnp.exp(lse - top) for lse in lses]
-        total = raised[0]
-        for one in raised[1:]:
-            total = total + one
-        shares = jnp.concatenate(raised + [total] * (HD // KVH - holders - 1), axis=0).T
-        for h in range(KVH):
-            cols = slice(h * HD, (h + 1) * HD)
-            mixed = tree_ref[r, :, cols].astype(F32) * shares[:, holders * KVH + h : holders * KVH + h + 1]
-            for p in range(holders):
-                share = shares[:, p * KVH + h : p * KVH + h + 1]
-                mixed = mixed + jnp.where(share > 0.0, home_ref[p, r, :, cols].astype(F32) * share, 0.0)
-            whole_sum = shares[:, (holders + 1) * KVH + h : (holders + 1) * KVH + h + 1]
-            mixed = (mixed / whole_sum).astype(BF16)
-            for t in range(TOPK):
-                start = t * ROWS + r * DRAFT
-                mixed_ref[start : start + DRAFT, cols] = mixed[t * DRAFT : (t + 1) * DRAFT]
-    buf_i = lax.broadcasted_iota(jnp.int32, (ROWS, BUF), 1)
-    placed = None
-    for t in range(TOPK):
-        pick = (buf_i == slots_ref[:, t : t + 1]).astype(F32).astype(BF16)
-        part = lax.dot_general(
-            pick, mixed_ref[t * ROWS : (t + 1) * ROWS, :], (((0,), (0,)), ((), ())), preferred_element_type=F32
-        )
-        placed = part if placed is None else placed + part
-    out_ref[...] = placed.astype(BF16)
-
-
-def mix(slots, home_out, home_lse, tree_out, tree_lse):
-    return pl.pallas_call(
-        mix_kernel,
+        parts = chip_parts(3, r) + [came(s) for s in ((4, 3), (2, 5))[r]]
+        parts.append((tree_buf.at[r], tree_lses[r], False))
+
+        def store(rows, values):
+            mixed_buf[r, rows] = values
+
+        merge_parts(parts, store)
+    for n in range(2):
+        cols = slice(n * HEADW // 2, (n + 1) * HEADW // 2)
+        total = None
+        for r in range(REQ_X):
+            spread = (buf_i == slot_rows_ref[r : r + 1, :]).astype(F32).astype(BF16)
+            part = lax.dot_general(spread, mixed_buf[r, cols], (((1,), (1,)), ((), ())), preferred_element_type=F32)
+            total = part if total is None else total + part
+        placed_ref[:, cols] = total.astype(BF16)
+    for copies in sib_copies + ring:
+        for one in copies:
+            one.wait_send()
+
+
+def bring_home(held_out, held_lse, queries, new_kv, reach_t, slot_rows):
+    chips = held_out.shape[0] // REQ_X // 2
+    part = (HEADW, QROWS)
+    rows = (KVH, QROWS)
+    return pl.pallas_call(
+        home_kernel,
         out_shape=jax.ShapeDtypeStruct((BUF, HEADW), BF16),
-        scratch_shapes=[VMEM((TOPK * ROWS, HEADW), BF16)],
-        name="mix",
-    )(slots, home_out, home_lse, tree_out, tree_lse)
+        scratch_shapes=[
+            VMEM((chips, REQ_X) + part, BF16),
+            VMEM((chips, REQ_X) + rows, F32),
+            VMEM((6,) + part, BF16),
+            VMEM((6,) + rows, F32),
+            VMEM((6,) + part, BF16),
+            VMEM((6,) + rows, F32),
+            VMEM((REQ_X,) + part, BF16),
+            VMEM((REQ_X,) + part, BF16),
+            DMA((2 * chips,)),
+            DMA((2 * chips,)),
+            DMA((12,)),
+            DMA((12,)),
+        ],
+        compiler_params=pltpu.CompilerParams(collective_id=0, has_side_effects=True),
+        name="bring_home",
+    )(held_out, held_lse, queries, new_kv, reach_t, slot_rows)
 
 
 def expert_out_kernel(parity_ref, mine_ref, theirs_ref, own_ref, other_ref, out_ref):
@@ -423,7 +513,6 @@
     parents,
     accepted_leaf,
 ):
-    holder_count = lax.axis_size("req")
     owner_index = lax.axis_index("req")
     parity = (lax.axis_index("exp") % 2).astype(jnp.int32).reshape(1)
     group_requests = page_count.shape[1]
@@ -433,7 +522,7 @@
     out_other = partner_half(w_out[0])
 
     choice = router_choice.reshape(ROWS, TOPK)
-    routed, normed, gates, slots = prologue(hidden_in.reshape(ROWS, D), choice, w_router)
+    routed, normed, gates, slots, slot_rows = prologue(hidden_in.reshape(ROWS, D), choice, w_router)
     arrived = exchange(routed)
     query_back = exchange(expert_query(parity, arrived, w_query[0], query_other))
 
@@ -470,14 +559,9 @@
     sorted_valid = remaining - sorted_pos * PAGE
 
     held_out, held_lse = attend_pages(order, sorted_request, sorted_valid, shared, kv_cache[0])
-    home_out = lax.all_to_all(
-        held_out.reshape(holder_count, REQ_X, QROWS, HEADW), "req", split_axis=0, concat_axis=0, tiled=True
-    )
-    home_lse = lax.all_to_all(
-        held_lse.reshape(holder_count, REQ_X, KVH, QROWS), "req", split_axis=0, concat_axis=0, tiled=True
-    )
-    tree_out, tree_lse = attend_tree(queries, new_kv, reachable)
-    placed = mix(slots, home_out, home_lse, tree_out, tree_lse)
+    reach_t = jnp.swapaxes(reachable, 1, 2)
+    reach_t = jnp.concatenate([reach_t] * TOPK, axis=-1)
+    placed = bring_home(held_out, held_lse, queries, new_kv, reach_t, slot_rows)
     out_back = exchange(expert_out(parity, exchange(placed), w_out[0], out_other))
     attn_out = combine(slots, gates, out_back).reshape(1, REQ_X, DRAFT, D)
 

time: 308 us -> 240 us (0.78)
  waiting for transfers between devices: 151 us -> 94.3 us
  blocking collectives: 9.57 us -> 0 us
  starting transfers between devices: 29 us -> 24 us
    all_to_all x1 -> x0, waiting for transfers between devices: 38.5 us -> none  [body(): lax.all_to_all(held_out.reshape(holder_count, REQ_X, QROWS, HEADW), 'req'...]
    all_gather x1, waiting for transfers between devices: 29.2 us -> 13.9 us  [body(): shared = lax.all_gather(queries, 'req', axis=0, tiled=True)]
    all_to_all x1 -> x0, blocking collectives: 9.57 us -> none  [body(): lax.all_to_all(held_lse.reshape(holder_count, REQ_X, KVH, QROWS), 'req',...]
    all_to_all x1 -> x0, starting transfers between devices: 4.54 us -> none  [body(): lax.all_to_all(held_out.reshape(holder_count, REQ_X, QROWS, HEADW), 'req'...]
    pallas_call x3 -> x2, Pallas kernels: 59.1 us -> 61.4 us  [the longest x1 32.2 us: attend_pages(): pl.pallas_call(page_kernel, out_shape=(jax.ShapeDtypeStruct((count, HEADW...]
  transfers between devices with their start and end apart: 10 -> 9, of which waited for: 8 -> 7; matrix products, arithmetic and copies ran while one was open for 3% -> 5% of each run, Pallas kernels for 7% -> 30%
where the time goes in v2:
time: 240 us; the launch traced here: 239 us
  waiting for transfers between devices  94.3 us (39%)
  Pallas kernels  89.3 us (37%)
  starting transfers between devices  24 us (10%)
  between operations  13.9 us (6%)
  local copies, waits for them, and re-layouts  11 us (5%)
  other arithmetic  4.14 us (2%)
    all_to_all x4, waiting for transfers between devices, exchange(): return lax.all_to_all(rows, 'exp', split_axis=0, concat_axis=0, tiled=True)  68.2 us
    pallas_call x1, Pallas kernels, attend_pages(): pl.pallas_call(page_kernel, out_shape=(jax.ShapeDtypeStruct((count, HEADW...  32.2 us
    pallas_call x1, Pallas kernels, bring_home(): pl.pallas_call(home_kernel, out_shape=jax.ShapeDtypeStruct((BUF, HEADW),...  29.2 us
    all_to_all x4, starting transfers between devices, exchange(): return lax.all_to_all(rows, 'exp', split_axis=0, concat_axis=0, tiled=True)  21.6 us
    all_gather x1, waiting for transfers between devices, body(): shared = lax.all_gather(queries, 'req', axis=0, tiled=True)  13.9 us
    ppermute x2, waiting for transfers between devices, partner_half(): lax.ppermute(piece, 'exp', [(i, i ^ 1) for i in range(lax.axis_size('exp'...  12.1 us
    unnamed x30, local copies, waits for them, and re-layouts  7.98 us
    pallas_call x1, Pallas kernels, project_kv(): pl.pallas_call(new_kv_kernel, out_shape=jax.ShapeDtypeStruct((ROWS, 2 * H...  6.35 us
  transfers between devices with their start and end apart: 9, of which 7 were waited for; matrix products, arithmetic and copies ran while one was open for 5% of the time, Pallas kernels for 30%

profile of v2, /device:TPU:0, one launch (start us, length us, event | category | flops | bytes accessed | tf_op | source)
XLA Modules:
  0.0 239.0 jit_solution(10998974715397746267)
XLA Ops:
  8.2 1.7 collective-permute-start
  9.8 6.3 %collective-permute-done = bf16[256,512]{1,0:T(8,128)(2,1)S(1)} collective-permute-done((bf16[256,512]{1,0:T(8,128)(2,1)S(1)}, bf16[256,512]{1,0:T(8,128)(2,1)S(1)}, u32[]{:S(2)}, u32[]{:S(2)}) %collective-permute-start) | collective-permute-done | bytes 262176 | tf_op jit(solution)/shard_map/ppermute | solution.py:494
  18.4 1.8 copy.47.router_ref
  20.2 3.5 %prologue.1 = (bf16[384,2048]{1,0:T(8,128)(2,1)}, bf16[128,2048]{1,0:T(8,128)(2,1)}, f32[128,2]{1,0:T(8,128)}, s32[128,2]{1,0:T(8,128)}, s32[2,128]{1,0:T(2,128)}) custom-call(bf16[128,2048]{1,0:T(8,128)(2,1)} %bitcast.60, s32[128,2]{1,0:T(8,128)} %copy.46.choice_ref, s32[2,128]{1,0:T(2,128)} %bitcast.62, bf16[2048,8]{1,0:T(8,128)(2,1)} %copy.47.router_ref), custom_call_target="tpu_custom_call" | custom-call | tf_op jit(solution)/shard_map/prologue/pallas_call | solution.py:86
  23.7 7.3 %all-to-all-start = ((bf16[16,24,2048]{2,1,0:T(8,128)(2,1)}), bf16[16,24,2048]{2,1,0:T(8,128)(2,1)S(1)}, u32[]{:S(2)}, u32[]{:S(2)}) async-start(bf16[16,24,2048]{2,1,0:T(8,128)(2,1)} %bitcast.58), calls=%async_computation | async-start | bytes 3145728 | tf_op jit(solution)/shard_map/all_to_all | solution.py:499
  32.5 21.2 %all-to-all-done = bf16[16,24,2048]{2,1,0:T(8,128)(2,1)S(1)} async-done(((bf16[16,24,2048]{2,1,0:T(8,128)(2,1)}), bf16[16,24,2048]{2,1,0:T(8,128)(2,1)S(1)}, u32[]{:S(2)}, u32[]{:S(2)}) %all-to-all-start) | async-done | bytes 1572896 | tf_op jit(solution)/shard_map/all_to_all | solution.py:499
  53.7 1.2 copy-done.2
  54.9 5.8 %expert_query.1 = bf16[384,1024]{1,0:T(8,128)(2,1)} custom-call(s32[1]{0:T(128)} %bitcast.2.parity_ref, bf16[384,2048]{1,0:T(8,128)(2,1)} %bitcast.50, bf16[2048,512]{1,0:T(8,128)(2,1)} %bitcast.56, bf16[2048,512]{1,0:T(8,128)(2,1)} %all-gather.4.cloned.1.call-done.other_ref), custom_call_target="tpu_custom_call" | custom-call | tf_op jit(solution)/shard_map/expert_query/pallas_call | solution.py:113
  60.7 3.6 %all-to-all-start.1 = ((bf16[16,24,1024]{2,1,0:T(8,128)(2,1)}), bf16[16,24,1024]{2,1,0:T(8,128)(2,1)S(1)}, u32[]{:S(2)}, u32[]{:S(2)}) async-start(bf16[16,24,1024]{2,1,0:T(8,128)(2,1)} %bitcast.55), calls=%async_computation.1 | async-start | bytes 1572864 | tf_op jit(solution)/shard_map/all_to_all | solution.py:499
  65.7 12.4 %all-to-all-done.1 = bf16[16,24,1024]{2,1,0:T(8,128)(2,1)S(1)} async-done(((bf16[16,24,1024]{2,1,0:T(8,128)(2,1)}), bf16[16,24,1024]{2,1,0:T(8,128)(2,1)S(1)}, u32[]{:S(2)}, u32[]{:S(2)}) %all-to-all-start.1) | async-done | bytes 786464 | tf_op jit(solution)/shard_map/all_to_all | solution.py:499
  79.0 2.8 %pick_rotate.1.query_ref = bf16[2,128,1024]{2,1,0:T(8,128)(2,1)} custom-call(s32[128,2]{1,0:T(8,128)} %get-tuple-element.9.slots_ref, f32[128,128]{1,0:T(8,128)} %get-tuple-element.26.cos_ref, f32[128,128]{1,0:T(8,128)} %get-tuple-element.27.sin_ref, bf16[384,1024]{1,0:T(8,128)(2,1)} %bitcast.54), custom_call_target="tpu_custom_call" | custom-call | tf_op jit(solution)/shard_map/pick_rotate/pallas_call | solution.py:146
  83.5 5.8 %collective-permute-done.1 = bf16[64,2048]{1,0:T(8,128)(2,1)S(1)} collective-permute-done((bf16[64,2048]{1,0:T(8,128)(2,1)S(1)}, bf16[64,2048]{1,0:T(8,128)(2,1)S(1)}, u32[]{:S(2)}, u32[]{:S(2)}) %collective-permute-start.1) | collective-permute-done | bytes 262176 | tf_op jit(solution)/shard_map/ppermute | solution.py:494
  90.0 6.3 %project_kv.1.kv_ref = bf16[128,2048]{1,0:T(8,128)(2,1)} custom-call(bf16[128,2048]{1,0:T(8,128)(2,1)} %get-tuple-element.14.normed_ref, bf16[2048,2048]{1,0:T(8,128)(2,1)} %weight_ref.1, f32[128,128]{1,0:T(8,128)} %get-tuple-element.26.cos_ref, f32[128,128]{1,0:T(8,128)} %get-tuple-element.27.sin_ref), custom_call_target="tpu_custom_call" | custom-call | flops 1073741824 | bytes 8388608 | tf_op jit(solution)/shard_map/project_kv/pallas_call | solution.py:171
  99.1 13.9 %all-gather.6.cloned.1.call-done.query_ref = bf16[16,128,1024]{2,1,0:T(8,128)(2,1)} async-done(((bf16[2,128,1024]{2,1,0:T(8,128)(2,1)}), bf16[16,128,1024]{2,1,0:T(8,128)(2,1)}) %all-gather.6.cloned.1.call-update) | async-done | bytes 4194320 | tf_op jit(solution)/shard_map/all_gather | solution.py:544
  113.0 32.2 %attend_pages.1 = (bf16[16,1024,128]{2,1,0:T(8,128)(2,1)}, f32[16,8,128]{2,1,0:T(8,128)}) custom-call(s32[16]{0:T(128)} %get-tuple-element.19.order_ref, s32[16]{0:T(128)} %copy-done.9, s32[16]{0:T(128)} %multiply_subtract_fusion.valid_ref, bf16[16,128,1024]{2,1,0:T(8,128)(2,1)} %all-gather.6.cloned.1.call-done.query_ref, bf16[16,128,2048]{2,1,0:T(8,128)(2,1)} %bitcast.46), custom_call_target="tpu_custom_call" | custom-call | tf_op jit(solution)/shard_map/attend_pages/pallas_call | solution.py:246
  145.2 29.2 %bring_home.1 = bf16[384,1024]{1,0:T(8,128)(2,1)} custom-call(bf16[16,1024,128]{2,1,0:T(8,128)(2,1)} %get-tuple-element.12.out_ref, f32[16,8,128]{2,1,0:T(8,128)} %get-tuple-element.13.lse_ref, bf16[2,128,1024]{2,1,0:T(8,128)(2,1)} %pick_rotate.1.query_ref, bf16[128,2048]{1,0:T(8,128)(2,1)} %project_kv.1.kv_ref, ...), custom_call_target="tpu_custom_call" | custom-call | tf_op jit(solution)/shard_map/bring_home/pallas_call | solution.py:409
  174.4 6.8 %all-to-all-start.2 = ((bf16[16,24,1024]{2,1,0:T(8,128)(2,1)}), bf16[16,24,1024]{2,1,0:T(8,128)(2,1)S(1)}, u32[]{:S(2)}, u32[]{:S(2)}) async-start(bf16[16,24,1024]{2,1,0:T(8,128)(2,1)} %bitcast.53), calls=%async_computation.2 | async-start | bytes 1572864 | tf_op jit(solution)/shard_map/all_to_all | solution.py:499
  181.3 13.8 %all-to-all-done.2 = bf16[16,24,1024]{2,1,0:T(8,128)(2,1)S(1)} async-done(((bf16[16,24,1024]{2,1,0:T(8,128)(2,1)}), bf16[16,24,1024]{2,1,0:T(8,128)(2,1)S(1)}, u32[]{:S(2)}, u32[]{:S(2)}) %all-to-all-start.2) | async-done | bytes 786464 | tf_op jit(solution)/shard_map/all_to_all | solution.py:499
  195.9 5.4 %expert_out.1 = bf16[384,2048]{1,0:T(8,128)(2,1)} custom-call(s32[1]{0:T(128)} %bitcast.2.parity_ref, bf16[384,1024]{1,0:T(8,128)(2,1)} %bitcast.47, bf16[384,1024]{1,0:T(8,128)(2,1)} %bitcast.48, bf16[512,2048]{1,0:T(8,128)(2,1)} %bitcast.57, bf16[512,2048]{1,0:T(8,128)(2,1)} %all-gather.8.cloned.1.call-done.other_ref), custom_call_target="tpu_custom_call" | custom-call | tf_op jit(solution)/shard_map/expert_out/pallas_call | solution.py:440
  201.4 3.8 %all-to-all-start.3 = ((bf16[16,24,2048]{2,1,0:T(8,128)(2,1)}), bf16[16,24,2048]{2,1,0:T(8,128)(2,1)S(1)}, u32[]{:S(2)}, u32[]{:S(2)}) async-start(bf16[16,24,2048]{2,1,0:T(8,128)(2,1)} %bitcast.51), calls=%async_computation.3 | async-start | bytes 3145728 | tf_op jit(solution)/shard_map/all_to_all | solution.py:499
  205.2 1.2 fusion
  206.5 20.8 %all-to-all-done.3 = bf16[16,24,2048]{2,1,0:T(8,128)(2,1)S(1)} async-done(((bf16[16,24,2048]{2,1,0:T(8,128)(2,1)}), bf16[16,24,2048]{2,1,0:T(8,128)(2,1)S(1)}, u32[]{:S(2)}, u32[]{:S(2)}) %all-to-all-start.3) | async-done | bytes 1572896 | tf_op jit(solution)/shard_map/all_to_all | solution.py:499
  227.3 1.1 copy-done.1
  228.5 4.0 %combine.1 = bf16[128,2048]{1,0:T(8,128)(2,1)} custom-call(s32[128,2]{1,0:T(8,128)} %get-tuple-element.9.slots_ref, f32[128,2]{1,0:T(8,128)} %get-tuple-element.10.gates_ref, bf16[384,2048]{1,0:T(8,128)(2,1)} %bitcast.49), custom_call_target="tpu_custom_call" | custom-call | tf_op jit(solution)/shard_map/combine/pallas_call | solution.py:470
  (65 shorter events, 13.0 us)
Async XLA Ops:
  7.2 46.6 %all-gather.4.cloned.1.call-start = ((), (), s32[]{:S(2)}) async-start(), calls=%async_computation.4 | async-start | bytes 2359296 | tf_op jit(solution)/shard_map/all_gather | solution.py:495
  8.2 8.0 %collective-permute-start = (bf16[256,512]{1,0:T(8,128)(2,1)S(1)}, bf16[256,512]{1,0:T(8,128)(2,1)S(1)}, u32[]{:S(2)}, u32[]{:S(2)}) collective-permute-start(bf16[256,512]{1,0:T(8,128)(2,1)S(1)} %dynamic-slice_bitcast_fusion.1), channel_id=1, source_target_pairs={{0,1},{1,0},{2,3},{3,2},{4,5},{5,4},{6,7},{7,6},{8,9},{9,8},{10,11... | collective-permute-start | bytes 786440 | tf_op jit(solution)/shard_map/ppermute | solution.py:494
  16.1 0.7 copy-start.5
  17.7 2.5 %copy-start.7 = (s32[128,2]{0,1:T(2,128)}, s32[128,2]{0,1:T(2,128)S(1)}, u32[]{:S(2)}) copy-start(s32[128,2]{0,1:T(2,128)S(1)} %reshape.130) | copy-start | bytes 3076
  20.2 10.8 %copy-start.8 = (s32[1,16]{1,0:T(1,128)S(1)}, s32[1,16]{1,0:T(1,128)}, u32[]{:S(2)}) copy-start(s32[1,16]{1,0:T(1,128)} %param.19) | copy-start | bytes 196
  20.2 11.1 %copy-start.12 = (s32[1,2]{1,0:T(1,128)S(1)}, s32[1,2]{1,0:T(1,128)}, u32[]{:S(2)}) copy-start(s32[1,2]{1,0:T(1,128)} %param.23) | copy-start | bytes 28
  20.2 11.2 %copy-start.10 = (s32[1,16]{1,0:T(1,128)S(1)}, s32[1,16]{1,0:T(1,128)}, u32[]{:S(2)}) copy-start(s32[1,16]{1,0:T(1,128)} %param.20) | copy-start | bytes 196
  20.2 11.2 %copy-start.11 = (s32[1,2,64]{2,1,0:T(2,128)S(1)}, s32[1,2,64]{2,1,0:T(2,128)}, u32[]{:S(2)}) copy-start(s32[1,2,64]{2,1,0:T(2,128)} %param.22) | copy-start | bytes 1540
  23.7 30.0 %all-to-all-start = ((bf16[16,24,2048]{2,1,0:T(8,128)(2,1)}), bf16[16,24,2048]{2,1,0:T(8,128)(2,1)S(1)}, u32[]{:S(2)}, u32[]{:S(2)}) async-start(bf16[16,24,2048]{2,1,0:T(8,128)(2,1)} %bitcast.58), calls=%async_computation | async-start | bytes 3145728 | tf_op jit(solution)/shard_map/all_to_all | solution.py:499
  53.7 1.2 copy-start.2
  60.7 17.4 %all-to-all-start.1 = ((bf16[16,24,1024]{2,1,0:T(8,128)(2,1)}), bf16[16,24,1024]{2,1,0:T(8,128)(2,1)S(1)}, u32[]{:S(2)}, u32[]{:S(2)}) async-start(bf16[16,24,1024]{2,1,0:T(8,128)(2,1)} %bitcast.55), calls=%async_computation.1 | async-start | bytes 1572864 | tf_op jit(solution)/shard_map/all_to_all | solution.py:499
  64.4 48.6 %all-gather.6.cloned.1.call-start = ((), (), s32[]{:S(2)}) async-start(), calls=%async_computation.5 | async-start | bytes 4718592 | tf_op jit(solution)/shard_map/all_gather | solution.py:544
  78.1 0.9 copy-start.4
  81.8 99.4 %all-gather.8.cloned.1.call-start = ((), (), s32[]{:S(2)}) async-start(), calls=%async_computation.6 | async-start | bytes 2359296 | tf_op jit(solution)/shard_map/all_gather | solution.py:495
  82.8 6.5 %collective-permute-start.1 = (bf16[64,2048]{1,0:T(8,128)(2,1)S(1)}, bf16[64,2048]{1,0:T(8,128)(2,1)S(1)}, u32[]{:S(2)}, u32[]{:S(2)}) collective-permute-start(bf16[64,2048]{1,0:T(8,128)(2,1)S(1)} %dynamic-slice_bitcast_fusion), channel_id=1, source_target_pairs={{0,1},{1,0},{2,3},{3,2},{4,5},{5,4},{6,7},{7,6},{8,9},{9,8},{10,11... | collective-permute-start | bytes 786440 | tf_op jit(solution)/shard_map/ppermute | solution.py:494
  89.3 0.7 copy-start.6
  90.0 6.4 %copy-start.13 = (s32[1,128]{1,0:T(1,128)S(1)}, s32[1,128]{1,0:T(1,128)}, u32[]{:S(2)}) copy-start(s32[1,128]{1,0:T(1,128)} %param.21) | copy-start | bytes 1540
  97.7 15.3 %copy-start.9 = (s32[16]{0:T(128)}, s32[16]{0:T(128)S(1)}, u32[]{:S(2)}) copy-start(s32[16]{0:T(128)S(1)} %convert_reduce_fusion.1.request_ref) | copy-start | bytes 196
  174.4 20.7 %all-to-all-start.2 = ((bf16[16,24,1024]{2,1,0:T(8,128)(2,1)}), bf16[16,24,1024]{2,1,0:T(8,128)(2,1)S(1)}, u32[]{:S(2)}, u32[]{:S(2)}) async-start(bf16[16,24,1024]{2,1,0:T(8,128)(2,1)} %bitcast.53), calls=%async_computation.2 | async-start | bytes 1572864 | tf_op jit(solution)/shard_map/all_to_all | solution.py:499
  195.0 0.9 copy-start
  201.4 3.9 %copy-start.3 = (bf16[128,2048]{1,0:T(8,128)(2,1)S(1)}, bf16[128,2048]{1,0:T(8,128)(2,1)}, u32[]{:S(2)}) copy-start(bf16[128,2048]{1,0:T(8,128)(2,1)} %project_kv.1.kv_ref) | copy-start | bytes 1572868
  201.4 25.9 %all-to-all-start.3 = ((bf16[16,24,2048]{2,1,0:T(8,128)(2,1)}), bf16[16,24,2048]{2,1,0:T(8,128)(2,1)S(1)}, u32[]{:S(2)}, u32[]{:S(2)}) async-start(bf16[16,24,2048]{2,1,0:T(8,128)(2,1)} %bitcast.51), calls=%async_computation.3 | async-start | bytes 3145728 | tf_op jit(solution)/shard_map/all_to_all | solution.py:499
  227.3 1.2 copy-start.1
Sparse Core Ops, SparseCore 0:
  17.0 28.0 all-gather.3
  81.9 31.0 all-gather.5
  114.7 25.1 all-gather.7
